TPU v7x, 128 devices: a whole 4x4x4 slice. The times are simulated.
128 devices in a mesh: grp: 4 (over x_lo, core), tile: 32 (over y, z, x_hi).
Axes of the slice: x: 4 (x_hi: 2, x_lo: 2; x = x_hi * 2 + x_lo), y: 4, z: 4, core: 2. Of those that a mesh axis runs over, the one named last changes fastest.
Arguments:
- raw: bfloat16 [16, 256, 15360], P('grp', 'tile'), may hold values from 0.25 to 4
- scales: bfloat16 [16, 64, 480], P('grp', 'tile'), may hold values from 0.29882812 to 1.1953125
- flat: float32 [256, 15360], P(None, 'tile'), may hold values from 0.25 to 1.75
- spectrum: float32 [32, 2, 256, 512], P('tile'), may hold values from -5 to 5
- pupil: float32 [2, 64, 128], replicated, may hold values from -5 to 5
- patterns: int32 [16, 4], replicated, may hold values from 0 to 31, all different within a row
- led_row: int32 [32], replicated, may hold values from 0 to 192
- led_col: int32 [32], replicated, may hold values from 0 to 384
Outputs:
- new_spectrum: float32 [32, 2, 256, 512], P('tile')
- stitched: float32 [2, 256, 15360], P(None, None, 'tile')
Inputs may be any that keep to these rules, and one draw needn't show every extreme that they name: `patterns`: each frame lights 4 different LEDs, and every LED is lit in some frame.
All inputs are finite; a program needn't handle non-finite values.
Results may differ from a plain program's by a relative error of at most 0.0003.
Values may be sent and summed in bfloat16 or wider, within the bound.
A program may use at most 128 MiB of HBM per device.

v0:
```python
import functools
import math

import jax
import jax.numpy as jnp
import ml_dtypes
import numpy as np
from jax import lax
from jax.experimental import pallas as pl
from jax.experimental.pallas import tpu as pltpu
from jax.sharding import PartitionSpec as P

TH = 256
TW = 512
OV = 32
BR = 4
BC = 32
PR = 64
PC = 128
FR_G = 4
LEDS = 4
HALF = TH // 2
HR = PR // 2
MARGIN = OV // 2
CORE = TW - OV
LANES = 128
BLOCKS = TW // LANES
MESH = pl.DeviceIdType.MESH
RB = HR + 8
STEP = 0.02
F32 = jnp.float32
BF16 = jnp.bfloat16


def split_np(table):
    hi = table.astype(ml_dtypes.bfloat16)
    lo = (table - hi.astype(np.float64)).astype(ml_dtypes.bfloat16)
    return hi, lo


def wave_np(length, band):
    places = np.arange(length)[:, None]
    freqs = np.arange(band)[None, :] - band // 2
    angle = (places * freqs % length) * (2.0 * np.pi / length)
    return np.cos(angle) / math.sqrt(band), np.sin(angle) / math.sqrt(band)


def object_tables():
    re, im = wave_np(TH, TH)
    rows = []
    for parity in (0, 1):
        a, b = re[:HALF, parity::2], im[:HALF, parity::2]
        rows.append(np.stack(split_np(np.block([[a, -b], [b, a]]))))
    re, im = (np.roll(part.T, -MARGIN, axis=1)[:TH] for part in wave_np(TW, TW))
    cols = np.stack([np.stack(split_np(re)), np.stack(split_np(im))], axis=1)
    return np.stack(rows), cols


def band_tables():
    col_re, col_im = (np.roll(part.T, -MARGIN, axis=1) for part in wave_np(TW, PC))
    cols = np.block([[col_re, col_im], [-col_im, col_re]])
    col_hi, col_lo = split_np(cols)
    row_re, row_im = wave_np(TH, PR)
    spread, gather = [], []
    for parity in (0, 1):
        re = row_re[:HALF, parity::2]
        im = row_im[:HALF, parity::2]
        rows_hi, rows_lo = split_np(np.block([[re, -im], [im, re]]))
        spread.append(np.concatenate([rows_hi, rows_hi, rows_lo, rows_lo], axis=1))
        gather.append(np.concatenate([rows_hi.T, rows_lo.T], axis=0))
    return np.stack([col_hi, col_lo]), np.stack(spread), np.stack(gather)


def split(x):
    hi = x.astype(BF16)
    return hi, (x - hi.astype(F32)).astype(BF16)


def dot(a, b):
    return jnp.dot(a, b, preferred_element_type=F32)


def dot_t(a, b):
    return lax.dot_general(a, b, (((1,), (1,)), ((), ())), preferred_element_type=F32)


def box_place(pat, lrow, lcol, frame, j):
    led = pat[frame, j]
    row = lrow[led]
    col = lcol[led]
    offset = col & 127
    lane = pl.multiple_of((col >> 7) * 128, 128)
    return row, offset, lane


def half_rows(row, parity):
    start = (row + parity) >> 1
    return pl.multiple_of((start >> 3) * 8, 8), start & 7, (row + parity) & 1


def load_halves(spec, pup, stage, sp, pd):
    sp[...] = jnp.zeros_like(sp)
    for c in (0, 1):
        for parity in (0, 1):
            for k in range(TW // 128):
                if parity == 0:
                    stage[c, k] = spec[c, :, k * 128 : (k + 1) * 128]
                sp[c, parity, :HALF, k * 128 : (k + 1) * 128] = stage[
                    c, k, pl.ds(parity, HALF, stride=2), :
                ]
            pd[c, parity] = pup[c, pl.ds(parity, HR, stride=2), :]


def forward_frame(frame, pat, lrow, lcol, sp, pd, cols, spread, lit, mid, field):
    for j in range(LEDS):
        row, offset, lane = box_place(pat, lrow, lcol, frame, j)
        back = (256 - offset) & 255
        for parity in (0, 1):
            base, shift, which = half_rows(row, parity)
            up = jnp.where(shift == 0, 0, RB - shift)
            box = [
                pltpu.roll(
                    pltpu.roll(sp[c, which, pl.ds(base, RB), pl.ds(lane, 256)], back, 1)[:, :PC],
                    up,
                    0,
                )[:HR]
                for c in (0, 1)
            ]
            p_re, p_im = pd[0, parity], pd[1, parity]
            rows = pl.ds(j * PR + parity * HR, HR)
            lit[rows, :PC] = p_re * box[0] - p_im * box[1]
            lit[rows, PC:] = p_re * box[1] + p_im * box[0]
    hi, lo = split(lit[...])
    mid[...] = dot(hi, cols[0]) + dot(lo, cols[0]) + dot(hi, cols[1])
    estimate = None
    for j in range(LEDS):
        parts = []
        for parity in (0, 1):
            rows = pl.ds(j * PR + parity * HR, HR)
            re_hi, re_lo = split(mid[rows, :TW])
            im_hi, im_lo = split(mid[rows, TW:])
            both = jnp.concatenate([re_hi, im_hi, re_lo, im_lo], axis=0)
            parts.append(dot(spread[parity], jnp.concatenate([both, both], axis=0)))
        upper = parts[0] + parts[1]
        lower = parts[0] - parts[1]
        field[j, 0, :HALF] = upper[:HALF]
        field[j, 0, HALF:] = lower[:HALF]
        field[j, 1, :HALF] = upper[HALF:]
        field[j, 1, HALF:] = lower[HALF:]
        power = jnp.concatenate(
            [
                upper[:HALF] * upper[:HALF] + upper[HALF:] * upper[HALF:],
                lower[:HALF] * lower[:HALF] + lower[HALF:] * lower[HALF:],
            ],
            axis=0,
        )
        estimate = power if estimate is None else estimate + power
    return estimate


def backward_frame(frame, misfit, pat, lrow, lcol, pd, cols, gather, field, low, acc):
    for j in range(LEDS):
        weighted = [misfit * field[j, c] for c in (0, 1)]
        for parity in (0, 1):
            mix = [
                w[:HALF] + w[HALF:] if parity == 0 else w[:HALF] - w[HALF:] for w in weighted
            ]
            hi, lo = split(jnp.concatenate(mix, axis=0))
            table = gather[parity]
            first = dot(table, hi)
            total = first[:PR] + first[PR:] + dot(table[:PR], lo)
            rows = pl.ds(j * PR + parity * HR, HR)
            low[rows, :TW] = total[:HR]
            low[rows, TW:] = total[HR:]
    hi, lo = split(low[...])
    grads = dot_t(hi, cols[0]) + dot_t(lo, cols[0]) + dot_t(hi, cols[1])
    for j in range(LEDS):
        row, offset, lane = box_place(pat, lrow, lcol, frame, j)
        for parity in (0, 1):
            base, shift, which = half_rows(row, parity)
            first = j * PR + parity * HR
            g_re = grads[first : first + HR, :PC]
            g_im = grads[first : first + HR, PC:]
            p_re, p_im = pd[0, parity], pd[1, parity]
            for c, value in (
                (0, p_re * g_re + p_im * g_im),
                (1, p_re * g_im - p_im * g_re),
            ):
                tall = jnp.concatenate([value, jnp.zeros((RB - HR, PC), F32)], axis=0)
                tall = pltpu.roll(tall, shift, 0)
                wide = jnp.concatenate([tall, jnp.zeros_like(tall)], axis=1)
                place = (c, which, pl.ds(base, RB), pl.ds(lane, 256))
                acc[place] += pltpu.roll(wide, offset, 1)


def gradient_kernel(
    pat, lrow, lcol, spec, pup, win, cols, spread, gather, out, stage, sp, pd, acc, lit, mid, field, low
):
    step = pl.program_id(0)
    frame = lax.axis_index("grp") * FR_G + step

    @pl.when(step == 0)
    def _():
        load_halves(spec, pup, stage, sp, pd)
        acc[...] = jnp.zeros_like(acc)

    estimate = forward_frame(frame, pat, lrow, lcol, sp, pd, cols, spread, lit, mid, field)
    misfit = estimate - win[0]
    backward_frame(frame, misfit, pat, lrow, lcol, pd, cols, gather, field, low, acc)

    @pl.when(step == FR_G - 1)
    def _():
        for c in (0, 1):
            for parity in (0, 1):
                for k in range(TW // 128):
                    out[k, c, pl.ds(parity, HALF, stride=2), :] = acc[
                        c, parity, :HALF, k * 128 : (k + 1) * 128
                    ]


def tile_gradient(spectrum, pupil, window, patterns, led_row, led_col):
    cols, spread, gather = (jnp.asarray(t) for t in band_tables())

    def whole(array):
        return pl.BlockSpec(array.shape, lambda s: (0,) * array.ndim)

    smem = pl.BlockSpec(memory_space=pltpu.SMEM)
    return pl.pallas_call(
        gradient_kernel,
        grid=(FR_G,),
        in_specs=[
            smem,
            smem,
            smem,
            whole(spectrum),
            whole(pupil),
            pl.BlockSpec((1, TH, TW), lambda s: (s, 0, 0)),
            whole(cols),
            whole(spread),
            whole(gather),
        ],
        out_specs=pl.BlockSpec((BLOCKS, 2, TH, LANES), lambda s: (0, 0, 0, 0)),
        out_shape=jax.ShapeDtypeStruct((BLOCKS, 2, TH, LANES), F32),
        scratch_shapes=[
            pltpu.VMEM((2, TW // 128, TH, 128), F32),
            pltpu.VMEM((2, 2, HALF + 8, TW + 128), F32),
            pltpu.VMEM((2, 2, HR, PC), F32),
            pltpu.VMEM((2, 2, HALF + 8, TW + 128), F32),
            pltpu.VMEM((LEDS * PR, 2 * PC), F32),
            pltpu.VMEM((LEDS * PR, 2 * TW), F32),
            pltpu.VMEM((LEDS, 2, TH, TW), F32),
            pltpu.VMEM((LEDS * PR, 2 * TW), F32),
        ],
        compiler_params=pltpu.CompilerParams(vmem_limit_bytes=48 * 2**20),
        name="gradient",
    )(patterns, led_row, led_col, spectrum, pupil, window, cols, spread, gather)


def build_columns(half, table):
    lane = lax.broadcasted_iota(jnp.int32, (1, TW), 1)
    sign = (1 - 2 * (lane & 1)).astype(F32)
    for i in (0, 1):
        rows = pl.ds(i * LANES, LANES)
        for h in (0, 1):
            re = half[h, 0, rows, :].astype(F32)
            im = half[h, 1, rows, :].astype(F32)
            for n, factor in ((0, None), (1, sign)):
                a = re if factor is None else re * factor
                b = im if factor is None else im * factor
                upper = pl.ds(n * LANES, LANES)
                lower = pl.ds((2 + n) * LANES, LANES)
                for k in range(BLOCKS):
                    cut = slice(k * LANES, (k + 1) * LANES)
                    table[i, h, k, upper, :LANES] = a[:, cut].astype(BF16)
                    table[i, h, k, upper, LANES:] = b[:, cut].astype(BF16)
                    table[i, h, k, lower, :LANES] = (-b[:, cut]).astype(BF16)
                    table[i, h, k, lower, LANES:] = a[:, cut].astype(BF16)


def object_rows(i, new, rows_table, lhs):
    parts = []
    for parity in (0, 1):
        data = [
            jnp.concatenate(
                [new[k, c, pl.ds(parity, HALF, stride=2), :] for k in (i, i + 2)], axis=1
            )
            for c in (0, 1)
        ]
        hi, lo = split(jnp.concatenate(data, axis=0))
        t_hi, t_lo = rows_table[parity, 0], rows_table[parity, 1]
        parts.append(dot(t_hi, hi) + dot(t_hi, lo) + dot(t_lo, hi))
    for n, value in enumerate((parts[0] + parts[1], parts[0] - parts[1])):
        hi, lo = split(value)
        rows = pl.ds(n * HALF, HALF)
        for h, part in enumerate((hi, lo)):
            lhs[h, rows, : 2 * LANES] = part[:HALF]
            lhs[h, rows, 2 * LANES :] = part[HALF:]


def object_block(i, k, lhs, table):
    hi, lo = lhs[0], lhs[1]
    return dot(hi, table[i, 0, k]) + dot(lo, table[i, 0, k]) + dot(hi, table[i, 1, k])


def pack_edge(value, first):
    lane = lax.broadcasted_iota(jnp.int32, (TH // 8, LANES), 1) // MARGIN
    packed = jnp.zeros((TH // 8, LANES), F32)
    for b in range(8):
        piece = value[b * 32 : (b + 1) * 32]
        piece = pltpu.roll(piece, (MARGIN * b - first) % LANES, 1)
        packed = jnp.where(lane == b, piece, packed)
    return packed


def unpack_edge(packed, first):
    return jnp.concatenate(
        [pltpu.roll(packed, (first - MARGIN * b) % LANES, 1) for b in range(8)], axis=0
    )


def finish_kernel(
    tiles,
    grad,
    spec,
    rows_table,
    half,
    fresh,
    stitched,
    got,
    pair,
    far,
    new,
    table,
    lhs,
    image,
    edge_out,
    edge_in,
    send,
    recv,
):
    group = lax.axis_index("grp")
    tile = lax.axis_index("tile")
    core = lax.rem(group, 2)
    mate = {"grp": group + 1 - 2 * core}
    partner = {"grp": group + 2 - 4 * lax.div(group, 2)}
    right = {"tile": lax.rem(tile + 1, tiles)}
    left = {"tile": lax.rem(tile + tiles - 1, tiles)}

    def remote(number, src, dst, device):
        return pltpu.make_async_remote_copy(
            src_ref=src,
            dst_ref=dst,
            send_sem=send.at[number],
            recv_sem=recv.at[number],
            device_id=device,
            device_id_type=MESH,
        )

    barrier = pltpu.get_barrier_semaphore()
    for device in (mate, partner, left, right):
        pl.semaphore_signal(barrier, inc=1, device_id=device, device_id_type=MESH)
    pl.semaphore_wait(barrier, 4)

    first = [remote(i, grad.at[2 - 2 * core + i], got.at[i], mate) for i in (0, 1)]
    for copy in first:
        copy.start()
    second = []
    for i in (0, 1):
        first[i].wait_recv()
        pair[i] = grad[2 * core + i] + got[i]
        second.append(remote(2 + i, pair.at[i], far.at[i], partner))
        second[i].start()
    build_columns(half, table)
    third = []
    for i in (0, 1):
        second[i].wait_recv()
        mine = 2 * core + i
        lanes = pl.ds(pl.multiple_of(mine * LANES, LANES), LANES)
        new[mine] = spec[:, :, lanes] - STEP * (pair[i] + far[i])
        third.append(remote(4 + i, new.at[mine], new.at[mine], mate))
        third[i].start()
        third[i].wait_recv()
        for k in (i, i + 2):
            fresh[:, :, k * LANES : (k + 1) * LANES] = new[k]
        object_rows(i, new, rows_table, lhs)
        if i == 0:
            for k in range(BLOCKS):
                image[k] = object_block(i, k, lhs, table)
    image[3] += object_block(1, 3, lhs, table)
    for c in (0, 1):
        value = image[3, :, c * LANES : (c + 1) * LANES]
        edge_out[0, c] = pack_edge(value, 96)
        edge_out[1, c] = pack_edge(value, 112)
    edges = [
        remote(6, edge_out.at[0], edge_in.at[0], right),
        remote(7, edge_out.at[1], edge_in.at[1], left),
    ]
    for copy in edges:
        copy.start()
    for k in range(BLOCKS - 1):
        image[k] += object_block(1, k, lhs, table)
    for c in (0, 1):
        for k in (1, 2):
            stitched[c, :, k * LANES : (k + 1) * LANES] = image[k, :, c * LANES : (c + 1) * LANES]
    lane = lax.broadcasted_iota(jnp.int32, (1, LANES), 1)
    place = lane.astype(F32)
    at_head = (lane < MARGIN) & (tile > 0)
    at_tail = (lane >= 80) & (lane < 96) & (tile < tiles - 1)
    for copy in edges:
        copy.wait_recv()
    for c in (0, 1):
        own = image[0, :, c * LANES : (c + 1) * LANES]
        other = unpack_edge(edge_in[0, c], 0)
        blend = own * ((place + 16.5) / OV) + other * ((15.5 - place) / OV)
        stitched[c, :, :LANES] = jnp.where(at_head, blend, own)
        own = image[3, :, c * LANES : (c + 1) * LANES]
        other = unpack_edge(edge_in[1, c], 80)
        blend = own * ((111.5 - place) / OV) + other * ((place - 79.5) / OV)
        stitched[c, :, 3 * LANES :] = jnp.where(at_tail, blend, own)[:, : CORE - 3 * LANES]
    for copy in first + second + third + edges:
        copy.wait_send()


def finish(grad, spectrum):
    rows_table, half = (jnp.asarray(t) for t in object_tables())
    vmem = pl.BlockSpec(memory_space=pltpu.VMEM)
    part = (2, TH, LANES)
    return pl.pallas_call(
        functools.partial(finish_kernel, lax.axis_size("tile")),
        in_specs=[vmem] * 4,
        out_specs=[vmem] * 2,
        out_shape=[
            jax.ShapeDtypeStruct((2, TH, TW), F32),
            jax.ShapeDtypeStruct((2, TH, CORE), F32),
        ],
        scratch_shapes=[
            pltpu.VMEM((2,) + part, F32),
            pltpu.VMEM((2,) + part, F32),
            pltpu.VMEM((2,) + part, F32),
            pltpu.VMEM((BLOCKS,) + part, F32),
            pltpu.VMEM((2, 2, BLOCKS, TW, 2 * LANES), BF16),
            pltpu.VMEM((2, TH, TW), BF16),
            pltpu.VMEM((BLOCKS, TH, 2 * LANES), F32),
            pltpu.VMEM((2, 2, TH // 8, LANES), F32),
            pltpu.VMEM((2, 2, TH // 8, LANES), F32),
            pltpu.SemaphoreType.DMA((8,)),
            pltpu.SemaphoreType.DMA((8,)),
        ],
        compiler_params=pltpu.CompilerParams(
            collective_id=1, has_side_effects=True, vmem_limit_bytes=48 * 2**20
        ),
        name="finish",
    )(grad, spectrum, rows_table, half)


def padded(block, sides, width):
    for axis, dim in sides:
        count = lax.axis_size(axis)
        forward = [(i, i + 1) for i in range(count - 1)]
        backward = [(target, source) for source, target in forward]
        low = lax.ppermute(
            lax.slice_in_dim(block, block.shape[dim] - width, None, axis=dim), axis, forward
        )
        high = lax.ppermute(lax.slice_in_dim(block, 0, width, axis=dim), axis, backward)
        block = jnp.concatenate([low, block, high], axis=dim)
    return block


def remove_tilt(flattened):
    rows_n = flattened.shape[1]
    cols_n = flattened.shape[2]
    ycentre = jnp.arange(rows_n, dtype=jnp.float32) - (rows_n - 1) / 2.0
    xcentre = jnp.arange(cols_n, dtype=jnp.float32) - (cols_n - 1) / 2.0
    slope_y = jnp.sum(flattened * ycentre[None, :, None], axis=(1, 2)) / (
        jnp.sum(ycentre * ycentre) * cols_n
    )
    slope_x = jnp.sum(flattened * xcentre[None, None, :], axis=(1, 2)) / (
        jnp.sum(xcentre * xcentre) * rows_n
    )
    return (
        flattened
        - slope_y[:, None, None] * ycentre[None, :, None]
        - slope_x[:, None, None] * xcentre[None, None, :]
    )


def spread_factors(coarse):
    return jnp.repeat(jnp.repeat(coarse.astype(jnp.float32), BR, axis=1), BC, axis=2)


def body(raw, scales, flat, spectrum, pupil, patterns, led_row, led_col):
    core = TW - OV
    margin = OV // 2
    tile_count = lax.axis_size("tile")
    rows_here = raw.shape[1]
    frames_here = raw.shape[0]
    dequant = raw.astype(jnp.float32) * spread_factors(scales)
    value_blocks = dequant.reshape(frames_here, rows_here, tile_count, core)
    arrived = lax.all_to_all(
        value_blocks.astype(jnp.bfloat16), "tile", split_axis=2, concat_axis=1, tiled=True
    ).astype(value_blocks.dtype)
    values = arrived.reshape(frames_here, TH, arrived.shape[-1])
    measured = remove_tilt(values * flat[None])
    window = padded(measured.astype(jnp.bfloat16), (("tile", 2),), margin).astype(measured.dtype)
    spectrum_tile = spectrum[0]
    window = jnp.roll(window, -margin, axis=2)
    local_total = tile_gradient(spectrum_tile, pupil, window, patterns, led_row, led_col)
    fresh, stitched = finish(local_total, spectrum_tile)
    return (fresh[None], stitched)


def solution(mesh):
    return jax.shard_map(
        body,
        mesh=mesh,
        in_specs=(
            P("grp", "tile", None),
            P("grp", "tile", None),
            P(None, "tile"),
            P("tile", None, None, None),
            P(),
            P(),
            P(),
            P(),
        ),
        out_specs=(P("tile", None, None, None), P(None, None, "tile")),
        check_vma=False,
    )
```

profile of v0, /device:TPU:1, one launch (start us, length us, event | category | flops | bytes accessed | tf_op | source)
XLA Modules:
  0.0 113.1 jit_solution(13553374723917008173)
XLA Ops:
  0.6 0.7 broadcast_in_dim.6
  1.4 4.9 %broadcast_in_dim.7 = f32[4,8,480,32]{3,2,1,0:T(8,128)} broadcast(f32[4,8,480]{2,1,0:T(8,128)S(1)} %reshape.90), dimensions={0,1,2} | broadcast | bytes 2027520 | tf_op jit(solution)/shard_map/broadcast_in_dim | solution.py:488
  6.3 5.9 %reshape.91 = f32[4,8,15360]{2,1,0:T(8,128)S(1)} reshape(f32[4,8,480,32]{3,2,1,0:T(8,128)} %broadcast_in_dim.7) | data formatting | bytes 3932160 | tf_op jit(solution)/shard_map/reshape | solution.py:488
  12.2 1.4 %multiply_convert_fusion = bf16[4,8,15360]{2,1,0:T(8,128)(2,1)S(1)} fusion(f32[4,8,15360]{2,1,0:T(8,128)S(1)} %reshape.91, bf16[4,8,15360]{2,1,0:T(8,128)(2,1)} %param.13), kind=kLoop, calls=%fused_computation.8 | loop fusion | flops 1474560 | bytes 3932160 | tf_op jit(solution)/shard_map/convert_element_type | solution.py:500
  13.6 1.8 %convert_element_type.42 = bf16[4,8,32,480]{3,2,1,0:T(8,128)(2,1)S(1)} reshape(bf16[4,8,15360]{2,1,0:T(8,128)(2,1)S(1)} %multiply_convert_fusion) | data formatting | bytes 1966080 | tf_op jit(solution)/shard_map/convert_element_type | solution.py:500
  15.4 1.5 %copy.25 = bf16[4,8,32,480]{3,1,0,2:T(8,128)(2,1)} copy(bf16[4,8,32,480]{3,2,1,0:T(8,128)(2,1)S(1)} %convert_element_type.42) | data formatting | bytes 1966080 | tf_op jit(solution)/shard_map/convert_element_type | solution.py:500
  16.9 11.3 %all-to-all-start = ((bf16[4,8,32,480]{3,1,0,2:T(8,128)(2,1)}), bf16[4,8,32,480]{3,1,0,2:T(8,128)(2,1)S(1)}, u32[]{:S(2)}, u32[]{:S(2)}) async-start(bf16[4,8,32,480]{3,1,0,2:T(8,128)(2,1)} %copy.25), calls=%async_computation | async-start | bytes 2097152 | tf_op jit(solution)/shard_map/all_to_all | solution.py:499
  28.5 0.6 multiply_reduce_fusion.2
  29.8 0.6 multiply_reduce_fusion.3
  31.1 15.4 %all-to-all-done = bf16[4,8,32,480]{3,1,0,2:T(8,128)(2,1)S(1)} async-done(((bf16[4,8,32,480]{3,1,0,2:T(8,128)(2,1)}), bf16[4,8,32,480]{3,1,0,2:T(8,128)(2,1)S(1)}, u32[]{:S(2)}, u32[]{:S(2)}) %all-to-all-start) | async-done | bytes 983072 | tf_op jit(solution)/shard_map/all_to_all | solution.py:499
  46.4 0.6 multiply_reduce_fusion.1
  47.2 0.4 fusion.2
  47.7 2.3 %collective-permute-start = (bf16[4,256,16]{2,1,0:T(8,128)(2,1)S(1)}, bf16[4,256,16]{2,1,0:T(8,128)(2,1)S(1)}, u32[]{:S(2)}, u32[]{:S(2)}) collective-permute-start(bf16[4,256,16]{2,1,0:T(8,128)(2,1)S(1)} %get-tuple-element.14), channel_id=1, source_target_pairs={{0,1},{1,2},{2,3},{3,4},{4,5},{5,6},{6,7},{7,8},{8,9},{9,10},{10,1... | collective-permute-start | bytes 98312 | tf_op jit(solution)/shard_map/ppermute | solution.py:461
  50.0 1.5 %collective-permute-start.1 = (bf16[4,256,16]{2,1,0:T(8,128)(2,1)S(1)}, bf16[4,256,16]{2,1,0:T(8,128)(2,1)S(1)}, u32[]{:S(2)}, u32[]{:S(2)}) collective-permute-start(bf16[4,256,16]{2,1,0:T(8,128)(2,1)S(1)} %get-tuple-element.15), channel_id=1, source_target_pairs={{1,0},{2,1},{3,2},{4,3},{5,4},{6,5},{7,6},{8,7},{9,8},{10,9},{11,1... | collective-permute-start | bytes 98312 | tf_op jit(solution)/shard_map/ppermute | solution.py:464
  51.6 1.7 %collective-permute-done = bf16[4,256,16]{2,1,0:T(8,128)(2,1)S(1)} collective-permute-done((bf16[4,256,16]{2,1,0:T(8,128)(2,1)S(1)}, bf16[4,256,16]{2,1,0:T(8,128)(2,1)S(1)}, u32[]{:S(2)}, u32[]{:S(2)}) %collective-permute-start) | collective-permute-done | bytes 32800 | tf_op jit(solution)/shard_map/ppermute | solution.py:461
  53.3 9.8 %collective-permute-done.1 = bf16[4,256,16]{2,1,0:T(8,128)(2,1)S(1)} collective-permute-done((bf16[4,256,16]{2,1,0:T(8,128)(2,1)S(1)}, bf16[4,256,16]{2,1,0:T(8,128)(2,1)S(1)}, u32[]{:S(2)}, u32[]{:S(2)}) %collective-permute-start.1) | collective-permute-done | bytes 32800 | tf_op jit(solution)/shard_map/ppermute | solution.py:464
  63.1 0.6 maximum_convert_fusion
  63.7 0.6 slice.20
  64.8 0.8 copy-done
  65.7 0.3 copy-done.2
  66.1 17.4 %gradient.1.grad = f32[4,2,256,128]{3,2,1,0:T(8,128)S(1)} custom-call(s32[16,4]{1,0:T(8,128)S(1)} %copy.29.pat, s32[32]{0:T(128)S(1)} %copy-done.7, s32[32]{0:T(128)S(1)} %copy-done.8, f32[2,256,512]{2,1,0:T(8,128)S(1)} %bitcast.26, f32[2,64,128]{2,1,0:T(8,128)S(1)} %copy-done.6, f32[4,256,512]{2,1,0:T(8,128)S(1)} %pad_maximum_fusion.win, ...), custom_call_target="tpu_custom_call" | custom-call | tf_op jit(solution)/shard_map/gradient/pallas_call | solution.py:228
  83.5 27.4 %finish.1 = (f32[2,256,512]{2,1,0:T(8,128)S(1)}, f32[2,256,480]{2,1,0:T(8,128)S(1)}) custom-call(f32[4,2,256,128]{3,2,1,0:T(8,128)S(1)} %gradient.1.grad, f32[2,256,512]{2,1,0:T(8,128)S(1)} %bitcast.27, bf16[2,2,256,256]{3,2,1,0:T(8,128)(2,1)S(1)} %copy-done.3, bf16[2,2,256,512]{3,2,1,0:T(8,128)(2,1)S(1)} %copy-done.1), custom_call_target="tpu_custom_call" | custom-call | tf_op jit(solution)/shard_map/finish/pallas_call | solution.py:428
  110.8 1.3 %copy.30 = f32[2,256,480]{1,2,0:T(8,128)} copy(f32[2,256,480]{2,1,0:T(8,128)S(1)} %get-tuple-element.11) | data formatting | bytes 1966080
  112.1 1.0 copy.33
  (32 shorter events, 1.2 us)
Async XLA Ops:
  15.4 12.9 %copy-start.9 = (f32[256,480]{0,1:T(8,128)S(1)}, f32[256,480]{0,1:T(8,128)}, u32[]{:S(2)}) copy-start(f32[256,480]{0,1:T(8,128)} %param.15) | copy-start | bytes 1474564
  16.9 29.5 %all-to-all-start = ((bf16[4,8,32,480]{3,1,0,2:T(8,128)(2,1)}), bf16[4,8,32,480]{3,1,0,2:T(8,128)(2,1)S(1)}, u32[]{:S(2)}, u32[]{:S(2)}) async-start(bf16[4,8,32,480]{3,1,0,2:T(8,128)(2,1)} %copy.25), calls=%async_computation | async-start | bytes 2097152 | tf_op jit(solution)/shard_map/all_to_all | solution.py:499
  47.1 4.4 %copy-start.10 = (s32[16,4]{0,1:T(4,128)S(1)}, s32[16,4]{0,1:T(4,128)}, u32[]{:S(2)}) copy-start(s32[16,4]{0,1:T(4,128)} %param.18) | copy-start | bytes 772
  47.7 5.6 %collective-permute-start = (bf16[4,256,16]{2,1,0:T(8,128)(2,1)S(1)}, bf16[4,256,16]{2,1,0:T(8,128)(2,1)S(1)}, u32[]{:S(2)}, u32[]{:S(2)}) collective-permute-start(bf16[4,256,16]{2,1,0:T(8,128)(2,1)S(1)} %get-tuple-element.14), channel_id=1, source_target_pairs={{0,1},{1,2},{2,3},{3,4},{4,5},{5,6},{6,7},{7,8},{8,9},{9,10},{10,1... | collective-permute-start | bytes 98312 | tf_op jit(solution)/shard_map/ppermute | solution.py:461
  50.0 13.1 %collective-permute-start.1 = (bf16[4,256,16]{2,1,0:T(8,128)(2,1)S(1)}, bf16[4,256,16]{2,1,0:T(8,128)(2,1)S(1)}, u32[]{:S(2)}, u32[]{:S(2)}) collective-permute-start(bf16[4,256,16]{2,1,0:T(8,128)(2,1)S(1)} %get-tuple-element.15), channel_id=1, source_target_pairs={{1,0},{2,1},{3,2},{4,3},{5,4},{6,5},{7,6},{8,7},{9,8},{10,9},{11,1... | collective-permute-start | bytes 98312 | tf_op jit(solution)/shard_map/ppermute | solution.py:464
  64.4 1.2 %copy-start = (f32[1,2,256,512]{3,2,1,0:T(8,128)S(1)}, f32[1,2,256,512]{3,2,1,0:T(8,128)}, u32[]{:S(2)}) copy-start(f32[1,2,256,512]{3,2,1,0:T(8,128)} %param.16) | copy-start | bytes 3145732
  64.4 1.5 %copy-start.2 = (bf16[2,256,1024]{2,1,0:T(8,128)(2,1)S(1)}, bf16[2,256,1024]{2,1,0:T(8,128)(2,1)}, u32[]{:S(2)}) copy-start(bf16[2,256,1024]{2,1,0:T(8,128)(2,1)} %constant.24.clone.cols) | copy-start | bytes 3145732
  64.5 1.6 %copy-start.4 = (bf16[2,256,256]{2,1,0:T(8,128)(2,1)S(1)}, bf16[2,256,256]{2,1,0:T(8,128)(2,1)}, u32[]{:S(2)}) copy-start(bf16[2,256,256]{2,1,0:T(8,128)(2,1)} %constant.25.clone.spread) | copy-start | bytes 786436
  64.5 1.6 %copy-start.5 = (bf16[2,128,256]{2,1,0:T(8,128)(2,1)S(1)}, bf16[2,128,256]{2,1,0:T(8,128)(2,1)}, u32[]{:S(2)}) copy-start(bf16[2,128,256]{2,1,0:T(8,128)(2,1)} %constant.26.clone.gather) | copy-start | bytes 393220
  64.5 1.6 %copy-start.6 = (f32[2,64,128]{2,1,0:T(8,128)S(1)}, f32[2,64,128]{2,1,0:T(8,128)}, u32[]{:S(2)}) copy-start(f32[2,64,128]{2,1,0:T(8,128)} %pup.1) | copy-start | bytes 196612
  64.5 1.6 %copy-start.7 = (s32[32]{0:T(128)S(1)}, s32[32]{0:T(128)}, u32[]{:S(2)}) copy-start(s32[32]{0:T(128)} %lrow.1) | copy-start | bytes 388
  64.5 1.6 %copy-start.8 = (s32[32]{0:T(128)S(1)}, s32[32]{0:T(128)}, u32[]{:S(2)}) copy-start(s32[32]{0:T(128)} %lcol.1) | copy-start | bytes 388
  66.1 17.4 %copy-start.1 = (bf16[2,2,256,512]{3,2,1,0:T(8,128)(2,1)S(1)}, bf16[2,2,256,512]{3,2,1,0:T(8,128)(2,1)}, u32[]{:S(2)}) copy-start(bf16[2,2,256,512]{3,2,1,0:T(8,128)(2,1)} %constant.28.clone.half) | copy-start | bytes 3145732
  66.1 17.4 %copy-start.3 = (bf16[2,2,256,256]{3,2,1,0:T(8,128)(2,1)S(1)}, bf16[2,2,256,256]{3,2,1,0:T(8,128)(2,1)}, u32[]{:S(2)}) copy-start(bf16[2,2,256,256]{3,2,1,0:T(8,128)(2,1)} %constant.27.clone.rows_table) | copy-start | bytes 1572868
where the time goes:
time: 114 us; the launch traced here: 113 us
  Pallas kernels  44.7 us (39%)
  waiting for transfers between devices  26.9 us (24%)
  local copies, waits for them, and re-layouts  19.5 us (17%)
  starting transfers between devices  15.1 us (13%)
  other arithmetic  4.75 us (4%)
  between operations  2.18 us (2%)
    pallas_call x1, Pallas kernels, finish(): pl.pallas_call(functools.partial(finish_kernel, lax.axis_size('tile')), i...  27.4 us
    pallas_call x1, Pallas kernels, tile_gradient(): pl.pallas_call(gradient_kernel, grid=(FR_G,), in_specs=[smem, smem, smem,...  17.4 us
    all_to_all x1, waiting for transfers between devices, body(): lax.all_to_all(value_blocks.astype(jnp.bfloat16), 'tile', split_axis=2, c...  15.4 us
    all_to_all x1, starting transfers between devices, body(): lax.all_to_all(value_blocks.astype(jnp.bfloat16), 'tile', split_axis=2, c...  11.3 us
    ppermute x1, waiting for transfers between devices, padded(): lax.ppermute(lax.slice_in_dim(block, 0, width, axis=dim), axis, backward)  9.8 us
    reshape x1, local copies, waits for them, and re-layouts, spread_factors(): jnp.repeat(jnp.repeat(coarse.astype(jnp.float32), BR, axis=1), BC, axis=2)  5.93 us
    broadcast_in_dim x1, local copies, waits for them, and re-layouts, spread_factors(): jnp.repeat(jnp.repeat(coarse.astype(jnp.float32), BR, axis=1), BC, axis=2)  4.94 us
    unnamed x26, local copies, waits for them, and re-layouts  3.81 us
  transfers between devices with their start and end apart: 3, of which 3 were waited for; matrix products, arithmetic and copies ran while one was open for 1% of the time, Pallas kernels for 0%

commit v1 on v0

--- a/solution.py
+++ b/solution.py
@@ -256,6 +256,247 @@
     )(patterns, led_row, led_col, spectrum, pupil, window, cols, spread, gather)
 
 
+def pack_edge(value, first):
+    lane = lax.broadcasted_iota(jnp.int32, (TH // 8, LANES), 1) // MARGIN
+    packed = jnp.zeros((TH // 8, LANES), F32)
+    for b in range(8):
+        piece = value[b * 32 : (b + 1) * 32]
+        piece = pltpu.roll(piece, (MARGIN * b - first) % LANES, 1)
+        packed = jnp.where(lane == b, piece, packed)
+    return packed
+
+
+def unpack_edge(packed, first):
+    return jnp.concatenate(
+        [pltpu.roll(packed, (first - MARGIN * b) % LANES, 1) for b in range(8)], axis=0
+    )
+
+
+def dequantize(raw, scales, dequant):
+    frames, rows, width = raw.shape
+    dequant[:, :LANES] = jnp.zeros((frames * rows, LANES), F32)
+    dequant[:, LANES + width :] = jnp.zeros((frames * rows, LANES), F32)
+    lane = lax.broadcasted_iota(jnp.int32, (rows, LANES), 1) // BC
+    upper = lax.broadcasted_iota(jnp.int32, (rows, LANES), 0) < BR
+    blocks = scales.shape[2]
+    per = LANES // BC
+    for first in range(0, blocks, LANES):
+        count = min(LANES, blocks - first)
+        for f in range(frames):
+            pair = scales[f, :, first : first + count].astype(F32)
+            if count < LANES:
+                pair = jnp.concatenate([pair, jnp.zeros((2, LANES - count), F32)], axis=1)
+            factors = jnp.where(
+                upper,
+                jnp.broadcast_to(pair[0:1], (rows, LANES)),
+                jnp.broadcast_to(pair[1:2], (rows, LANES)),
+            )
+            for k in range(count // per):
+                column = (first // per + k) * LANES
+                spread = jnp.take_along_axis(factors, lane + per * k, axis=1)
+                codes = raw[f, :, column : column + LANES].astype(F32)
+                dequant[f * rows : (f + 1) * rows, LANES + column : 2 * LANES + column] = (
+                    codes * spread
+                )
+
+
+def cut_message(dequant, tile):
+    start = CORE * tile - MARGIN + LANES
+    aligned = pl.multiple_of(start // LANES * LANES, LANES)
+    offset = start - aligned + MARGIN
+    wide = dequant[:, pl.ds(aligned, TW + LANES)]
+    wide = pltpu.roll(wide, TW + LANES - offset, 1)
+    lane = lax.broadcasted_iota(jnp.int32, (1, LANES), 1)
+    last = jnp.where(lane < LANES - MARGIN, wide[:, TW - LANES : TW], wide[:, TW:])
+    return jnp.concatenate([wide[:, : TW - LANES], last], axis=1).astype(BF16)
+
+
+def centred():
+    y = lax.broadcasted_iota(jnp.int32, (TH, 1), 0).astype(F32) - (TH - 1) / 2.0
+    lane = lax.broadcasted_iota(jnp.int32, (1, TW), 1)
+    x = lane.astype(F32) - (CORE - 1) / 2.0
+    return y, x, lane
+
+
+Y_NORM = float(np.sum((np.arange(TH) - (TH - 1) / 2.0) ** 2) * CORE)
+X_NORM = float(np.sum((np.arange(CORE) - (CORE - 1) / 2.0) ** 2) * TH)
+
+
+def measure_kernel(
+    tiles,
+    raw,
+    scales,
+    flat,
+    window,
+    dequant,
+    message,
+    arrived,
+    gains,
+    flat_out,
+    flat_in,
+    slope_out,
+    slope_in,
+    send,
+    recv,
+    side_send,
+    side_recv,
+):
+    frames = raw.shape[0]
+    rows = raw.shape[1]
+    tile = lax.axis_index("tile")
+    right = {"tile": lax.rem(tile + 1, tiles)}
+    left = {"tile": lax.rem(tile + tiles - 1, tiles)}
+
+    def side(number, src, dst, device):
+        return pltpu.make_async_remote_copy(
+            src_ref=src,
+            dst_ref=dst,
+            send_sem=side_send.at[number],
+            recv_sem=side_recv.at[number],
+            device_id=device,
+            device_id_type=MESH,
+        )
+
+    def block(source, target):
+        return pltpu.make_async_remote_copy(
+            src_ref=message.at[target],
+            dst_ref=arrived.at[source],
+            send_sem=send.at[target],
+            recv_sem=recv.at[source],
+            device_id={"tile": target},
+            device_id_type=MESH,
+        )
+
+    barrier = pltpu.get_barrier_semaphore()
+
+    @pl.loop(1, tiles)
+    def _(i):
+        pl.semaphore_signal(
+            barrier, inc=1, device_id={"tile": lax.rem(tile + i, tiles)}, device_id_type=MESH
+        )
+
+    dequantize(raw, scales, dequant)
+    tail = jnp.concatenate(
+        [flat[:, 3 * LANES :], jnp.zeros((TH, TW - CORE), F32)], axis=1
+    )
+    flat_out[0] = pack_edge(tail, 80)
+    flat_out[1] = pack_edge(flat[:, :LANES], 0)
+    pl.semaphore_wait(barrier, tiles - 1)
+
+    @pl.loop(1, tiles)
+    def _(i):
+        target = lax.rem(tile + i, tiles)
+        message[target] = cut_message(dequant, target)
+        block(tile, target).start()
+
+    arrived[tile] = cut_message(dequant, tile)
+    flats = [side(0, flat_out.at[0], flat_in.at[0], right), side(1, flat_out.at[1], flat_in.at[1], left)]
+    for copy in flats:
+        copy.start()
+    y, x, lane = centred()
+    edge = lane[:, 3 * LANES :]
+    for copy in flats:
+        copy.wait_recv()
+    gains[:, : 3 * LANES] = flat[:, : 3 * LANES]
+    outer = jnp.where(
+        edge < CORE + MARGIN, unpack_edge(flat_in[1], 96), unpack_edge(flat_in[0], 112)
+    )
+    gains[:, 3 * LANES :] = jnp.where(edge < CORE, tail, outer)
+
+    @pl.loop(1, tiles + 1)
+    def _(i):
+        source = lax.rem(tile + tiles - i, tiles)
+
+        @pl.when(i < tiles)
+        def _():
+            block(source, tile).wait_recv()
+
+        here = pl.ds(pl.multiple_of(source * rows, rows), rows)
+        values = arrived[source].astype(F32)
+        for f in range(frames):
+            window[f, here, :] = values[f * rows : (f + 1) * rows] * gains[here, :]
+
+    inside = (lane < CORE).astype(F32)
+    slopes = []
+    for f in range(frames):
+        flattened = window[f]
+        columns = jnp.sum(flattened, axis=0, keepdims=True)
+        tilted = jnp.sum(flattened * y, axis=0, keepdims=True)
+        slope_y = jnp.sum(tilted * inside, axis=1, keepdims=True) / Y_NORM
+        slope_x = jnp.sum(columns * (x * inside), axis=1, keepdims=True) / X_NORM
+        slopes.append((slope_y, slope_x))
+        slope_out[f : f + 1] = jnp.broadcast_to(slope_y, (1, LANES))
+        slope_out[frames + f : frames + f + 1] = jnp.broadcast_to(slope_x, (1, LANES))
+    copies = [side(2, slope_out, slope_in.at[0], right), side(3, slope_out, slope_in.at[1], left)]
+    for copy in copies:
+        copy.start()
+    for f in range(frames):
+        slope_y, slope_x = slopes[f]
+        for k in range(BLOCKS - 1):
+            cut = slice(k * LANES, (k + 1) * LANES)
+            window[f, :, cut] = window[f, :, cut] - slope_y * y - slope_x * x[:, cut]
+    for copy in copies:
+        copy.wait_recv()
+    x_edge = x[:, 3 * LANES :]
+    own = edge < CORE
+    after = edge < CORE + MARGIN
+    blank = ((~own) & after & (tile == tiles - 1)) | ((~after) & (tile == 0))
+    for f in range(frames):
+        slope_y, slope_x = slopes[f]
+        row_y = jnp.where(
+            own, slope_y, jnp.where(after, slope_in[1, f : f + 1], slope_in[0, f : f + 1])
+        )
+        row_x = jnp.where(
+            own,
+            slope_x * x_edge,
+            jnp.where(
+                after,
+                slope_in[1, frames + f : frames + f + 1] * (x_edge - CORE),
+                slope_in[0, frames + f : frames + f + 1] * (x_edge - 32.0),
+            ),
+        )
+        value = window[f, :, 3 * LANES :] - row_y * y - row_x
+        window[f, :, 3 * LANES :] = jnp.where(blank, 0.0, value)
+    for copy in flats + copies:
+        copy.wait_send()
+
+    @pl.loop(1, tiles)
+    def _(i):
+        block(tile, lax.rem(tile + i, tiles)).wait_send()
+
+
+def measure(raw, scales, flat):
+    vmem = pl.BlockSpec(memory_space=pltpu.VMEM)
+    tiles = lax.axis_size("tile")
+    frames, rows, width = raw.shape
+    deep = frames * rows
+    small = (TH // 8, LANES)
+    return pl.pallas_call(
+        functools.partial(measure_kernel, tiles),
+        in_specs=[vmem] * 3,
+        out_specs=vmem,
+        out_shape=jax.ShapeDtypeStruct((frames, TH, TW), F32),
+        scratch_shapes=[
+            pltpu.VMEM((deep, width + 2 * LANES), F32),
+            pltpu.VMEM((tiles, deep, TW), BF16),
+            pltpu.VMEM((tiles, deep, TW), BF16),
+            pltpu.VMEM((TH, TW), F32),
+            pltpu.VMEM((2,) + small, F32),
+            pltpu.VMEM((2,) + small, F32),
+            pltpu.VMEM((2 * frames, LANES), F32),
+            pltpu.VMEM((2, 2 * frames, LANES), F32),
+            pltpu.SemaphoreType.DMA((tiles,)),
+            pltpu.SemaphoreType.DMA((tiles,)),
+            pltpu.SemaphoreType.DMA((4,)),
+            pltpu.SemaphoreType.DMA((4,)),
+        ],
+        compiler_params=pltpu.CompilerParams(
+            collective_id=2, has_side_effects=True, vmem_limit_bytes=48 * 2**20
+        ),
+        name="measure",
+    )(raw, scales, flat)
+
+
 def build_columns(half, table):
     lane = lax.broadcasted_iota(jnp.int32, (1, TW), 1)
     sign = (1 - 2 * (lane & 1)).astype(F32)
@@ -300,22 +541,6 @@
 def object_block(i, k, lhs, table):
     hi, lo = lhs[0], lhs[1]
     return dot(hi, table[i, 0, k]) + dot(lo, table[i, 0, k]) + dot(hi, table[i, 1, k])
-
-
-def pack_edge(value, first):
-    lane = lax.broadcasted_iota(jnp.int32, (TH // 8, LANES), 1) // MARGIN
-    packed = jnp.zeros((TH // 8, LANES), F32)
-    for b in range(8):
-        piece = value[b * 32 : (b + 1) * 32]
-        piece = pltpu.roll(piece, (MARGIN * b - first) % LANES, 1)
-        packed = jnp.where(lane == b, piece, packed)
-    return packed
-
-
-def unpack_edge(packed, first):
-    return jnp.concatenate(
-        [pltpu.roll(packed, (first - MARGIN * b) % LANES, 1) for b in range(8)], axis=0
-    )
 
 
 def finish_kernel(
@@ -453,57 +678,9 @@
     )(grad, spectrum, rows_table, half)
 
 
-def padded(block, sides, width):
-    for axis, dim in sides:
-        count = lax.axis_size(axis)
-        forward = [(i, i + 1) for i in range(count - 1)]
-        backward = [(target, source) for source, target in forward]
-        low = lax.ppermute(
-            lax.slice_in_dim(block, block.shape[dim] - width, None, axis=dim), axis, forward
-        )
-        high = lax.ppermute(lax.slice_in_dim(block, 0, width, axis=dim), axis, backward)
-        block = jnp.concatenate([low, block, high], axis=dim)
-    return block
-
-
-def remove_tilt(flattened):
-    rows_n = flattened.shape[1]
-    cols_n = flattened.shape[2]
-    ycentre = jnp.arange(rows_n, dtype=jnp.float32) - (rows_n - 1) / 2.0
-    xcentre = jnp.arange(cols_n, dtype=jnp.float32) - (cols_n - 1) / 2.0
-    slope_y = jnp.sum(flattened * ycentre[None, :, None], axis=(1, 2)) / (
-        jnp.sum(ycentre * ycentre) * cols_n
-    )
-    slope_x = jnp.sum(flattened * xcentre[None, None, :], axis=(1, 2)) / (
-        jnp.sum(xcentre * xcentre) * rows_n
-    )
-    return (
-        flattened
-        - slope_y[:, None, None] * ycentre[None, :, None]
-        - slope_x[:, None, None] * xcentre[None, None, :]
-    )
-
-
-def spread_factors(coarse):
-    return jnp.repeat(jnp.repeat(coarse.astype(jnp.float32), BR, axis=1), BC, axis=2)
-
-
 def body(raw, scales, flat, spectrum, pupil, patterns, led_row, led_col):
-    core = TW - OV
-    margin = OV // 2
-    tile_count = lax.axis_size("tile")
-    rows_here = raw.shape[1]
-    frames_here = raw.shape[0]
-    dequant = raw.astype(jnp.float32) * spread_factors(scales)
-    value_blocks = dequant.reshape(frames_here, rows_here, tile_count, core)
-    arrived = lax.all_to_all(
-        value_blocks.astype(jnp.bfloat16), "tile", split_axis=2, concat_axis=1, tiled=True
-    ).astype(value_blocks.dtype)
-    values = arrived.reshape(frames_here, TH, arrived.shape[-1])
-    measured = remove_tilt(values * flat[None])
-    window = padded(measured.astype(jnp.bfloat16), (("tile", 2),), margin).astype(measured.dtype)
+    window = measure(raw, scales, flat)
     spectrum_tile = spectrum[0]
-    window = jnp.roll(window, -margin, axis=2)
     local_total = tile_gradient(spectrum_tile, pupil, window, patterns, led_row, led_col)
     fresh, stitched = finish(local_total, spectrum_tile)
     return (fresh[None], stitched)

time: 114 us -> 84.1 us (0.74)
  Pallas kernels: 44.7 us -> 76.7 us
  waiting for transfers between devices: 26.9 us -> 0 us
  starting transfers between devices: 15.1 us -> 0 us
  local copies, waits for them, and re-layouts: 19.5 us -> 6.31 us
  other arithmetic: 4.75 us -> 0 us
  between operations: 2.18 us -> 0.77 us
    pallas_call x0 -> x1, Pallas kernels: none -> 32 us  [measure(): pl.pallas_call(functools.partial(measure_kernel, tiles), in_specs=[vmem]...]
    all_to_all x1 -> x0, waiting for transfers between devices: 15.4 us -> none  [body(): lax.all_to_all(value_blocks.astype(jnp.bfloat16), 'tile', split_axis=2, c...]
    ppermute x2 -> x0, waiting for transfers between devices: 11.5 us -> none  [the longest x1 9.8 us: padded(): lax.ppermute(lax.slice_in_dim(block, 0, width, axis=dim), axis, backward)]
    all_to_all x1 -> x0, starting transfers between devices: 11.3 us -> none  [body(): lax.all_to_all(value_blocks.astype(jnp.bfloat16), 'tile', split_axis=2, c...]
    reshape x2 -> x0, local copies, waits for them, and re-layouts: 5.95 us -> none  [the longest x1 5.93 us: spread_factors(): jnp.repeat(jnp.repeat(coarse.astype(jnp.float32), BR, axis=1), BC, axis=2)]
    broadcast_in_dim x2 -> x0, local copies, waits for them, and re-layouts: 5.65 us -> none  [the longest x1 4.94 us: spread_factors(): jnp.repeat(jnp.repeat(coarse.astype(jnp.float32), BR, axis=1), BC, axis=2)]
    ppermute x2 -> x0, starting transfers between devices: 3.76 us -> none  [the longest x1 2.29 us: padded(): lax.ppermute(lax.slice_in_dim(block, block.shape[dim] - width, None, axis...]
    convert_element_type x2 -> x0, local copies, waits for them, and re-layouts: 3.31 us -> none  [body(): value_blocks.astype(jnp.bfloat16)]
  transfers between devices with their start and end apart: 3 -> 0, of which waited for: 3 -> 0; matrix products, arithmetic and copies ran while one was open for 1% -> 0% of each run, Pallas kernels for 0% -> 0%
where the time goes in v1:
time: 84.1 us; the launch traced here: 83.8 us
  Pallas kernels  76.7 us (91%)
  local copies, waits for them, and re-layouts  6.31 us (8%)
    pallas_call x1, Pallas kernels, measure(): pl.pallas_call(functools.partial(measure_kernel, tiles), in_specs=[vmem]...  32 us
    pallas_call x1, Pallas kernels, finish(): pl.pallas_call(functools.partial(finish_kernel, lax.axis_size('tile')), i...  27.4 us
    pallas_call x1, Pallas kernels, tile_gradient(): pl.pallas_call(gradient_kernel, grid=(FR_G,), in_specs=[smem, smem, smem,...  17.4 us
    unnamed x26, local copies, waits for them, and re-layouts  6.31 us

profile of v1, /device:TPU:1, one launch (start us, length us, event | category | flops | bytes accessed | tf_op | source)
XLA Modules:
  0.0 83.8 jit_solution(17311332938370013248)
XLA Ops:
  0.6 0.8 copy.16.pat
  1.4 0.0 copy-start
  1.4 0.0 copy-start.2
  1.4 1.4 %copy.15.flat = f32[256,480]{1,0:T(8,128)S(1)} copy(f32[256,480]{0,1:T(8,128)} %param.15) | data formatting | bytes 983040 | tf_op args[2]
  2.8 0.0 copy-start.3
  2.8 1.2 %copy-done.3 = bf16[4,8,15360]{2,1,0:T(8,128)(2,1)S(1)} copy-done((bf16[4,8,15360]{2,1,0:T(8,128)(2,1)S(1)}, bf16[4,8,15360]{2,1,0:T(8,128)(2,1)}, u32[]{:S(2)}) %copy-start.3) | copy-done | bytes 983064
  4.0 0.7 copy-done.8
  4.7 0.0 copy-start.10
  4.7 32.0 %measure.1.win = f32[4,256,512]{2,1,0:T(8,128)S(1)} custom-call(bf16[4,8,15360]{2,1,0:T(8,128)(2,1)S(1)} %copy-done.3, bf16[4,2,480]{2,1,0:T(2,128)(2,1)S(1)} %copy-done.8, f32[256,480]{1,0:T(8,128)S(1)} %copy.15.flat), custom_call_target="tpu_custom_call" | custom-call | tf_op jit(solution)/shard_map/measure/pallas_call | solution.py:474
  36.7 0.0 copy-done
  36.7 0.0 copy-done.2
  36.7 0.0 copy-done.5
  36.7 0.0 copy-done.6
  36.8 0.0 copy-done.7
  36.8 0.0 copy-done.9
  36.8 0.0 copy-done.10
  36.8 0.0 copy-start.1
  36.8 0.0 copy-start.4
  36.8 17.4 %gradient.1.grad = f32[4,2,256,128]{3,2,1,0:T(8,128)S(1)} custom-call(s32[16,4]{1,0:T(8,128)S(1)} %copy.16.pat, s32[32]{0:T(128)S(1)} %copy-done.9, s32[32]{0:T(128)S(1)} %copy-done.10, f32[2,256,512]{2,1,0:T(8,128)S(1)} %bitcast.2, f32[2,64,128]{2,1,0:T(8,128)S(1)} %copy-done.7, f32[4,256,512]{2,1,0:T(8,128)S(1)} %measure.1.win, ...), custom_call_target="tpu_custom_call" | custom-call | tf_op jit(solution)/shard_map/gradient/pallas_call | solution.py:228
  54.2 0.0 copy-done.1
  54.2 0.0 copy-done.4
  54.2 27.4 %finish.1 = (f32[2,256,512]{2,1,0:T(8,128)S(1)}, f32[2,256,480]{2,1,0:T(8,128)S(1)}) custom-call(f32[4,2,256,128]{3,2,1,0:T(8,128)S(1)} %gradient.1.grad, f32[2,256,512]{2,1,0:T(8,128)S(1)} %bitcast.3, bf16[2,2,256,256]{3,2,1,0:T(8,128)(2,1)S(1)} %copy-done.4, bf16[2,2,256,512]{3,2,1,0:T(8,128)(2,1)S(1)} %copy-done.1), custom_call_target="tpu_custom_call" | custom-call | tf_op jit(solution)/shard_map/finish/pallas_call | solution.py:653
  81.6 1.3 %copy.17 = f32[2,256,480]{1,2,0:T(8,128)} copy(f32[2,256,480]{2,1,0:T(8,128)S(1)} %get-tuple-element.7) | data formatting | bytes 1966080
  82.8 1.0 %copy.19 = f32[1,2,256,512]{3,2,1,0:T(8,128)} copy(f32[1,2,256,512]{3,2,1,0:T(8,128)S(1)} %bitcast.4) | data formatting | bytes 2097152
  (5 shorter events, 0.0 us)
Async XLA Ops:
  1.4 35.3 %copy-start = (f32[1,2,256,512]{3,2,1,0:T(8,128)S(1)}, f32[1,2,256,512]{3,2,1,0:T(8,128)}, u32[]{:S(2)}) copy-start(f32[1,2,256,512]{3,2,1,0:T(8,128)} %param.16) | copy-start | bytes 3145732
  1.4 35.3 %copy-start.2 = (bf16[2,256,1024]{2,1,0:T(8,128)(2,1)S(1)}, bf16[2,256,1024]{2,1,0:T(8,128)(2,1)}, u32[]{:S(2)}) copy-start(bf16[2,256,1024]{2,1,0:T(8,128)(2,1)} %constant.10.clone.cols) | copy-start | bytes 3145732
  2.8 1.2 %copy-start.3 = (bf16[4,8,15360]{2,1,0:T(8,128)(2,1)S(1)}, bf16[4,8,15360]{2,1,0:T(8,128)(2,1)}, u32[]{:S(2)}) copy-start(bf16[4,8,15360]{2,1,0:T(8,128)(2,1)} %raw.1) | copy-start | bytes 2949124
  4.0 0.7 copy-start.8
  4.7 32.1 %copy-start.5 = (bf16[2,256,256]{2,1,0:T(8,128)(2,1)S(1)}, bf16[2,256,256]{2,1,0:T(8,128)(2,1)}, u32[]{:S(2)}) copy-start(bf16[2,256,256]{2,1,0:T(8,128)(2,1)} %constant.11.clone.spread) | copy-start | bytes 786436
  4.7 32.1 %copy-start.6 = (bf16[2,128,256]{2,1,0:T(8,128)(2,1)S(1)}, bf16[2,128,256]{2,1,0:T(8,128)(2,1)}, u32[]{:S(2)}) copy-start(bf16[2,128,256]{2,1,0:T(8,128)(2,1)} %constant.12.clone.gather) | copy-start | bytes 393220
  4.7 32.1 %copy-start.7 = (f32[2,64,128]{2,1,0:T(8,128)S(1)}, f32[2,64,128]{2,1,0:T(8,128)}, u32[]{:S(2)}) copy-start(f32[2,64,128]{2,1,0:T(8,128)} %pup.1) | copy-start | bytes 196612
  4.7 32.1 %copy-start.9 = (s32[32]{0:T(128)S(1)}, s32[32]{0:T(128)}, u32[]{:S(2)}) copy-start(s32[32]{0:T(128)} %lrow.1) | copy-start | bytes 388
  4.7 32.1 %copy-start.10 = (s32[32]{0:T(128)S(1)}, s32[32]{0:T(128)}, u32[]{:S(2)}) copy-start(s32[32]{0:T(128)} %lcol.1) | copy-start | bytes 388
  36.8 17.4 %copy-start.1 = (bf16[2,2,256,512]{3,2,1,0:T(8,128)(2,1)S(1)}, bf16[2,2,256,512]{3,2,1,0:T(8,128)(2,1)}, u32[]{:S(2)}) copy-start(bf16[2,2,256,512]{3,2,1,0:T(8,128)(2,1)} %constant.14.clone.half) | copy-start | bytes 3145732
  36.8 17.4 %copy-start.4 = (bf16[2,2,256,256]{3,2,1,0:T(8,128)(2,1)S(1)}, bf16[2,2,256,256]{3,2,1,0:T(8,128)(2,1)}, u32[]{:S(2)}) copy-start(bf16[2,2,256,256]{3,2,1,0:T(8,128)(2,1)} %constant.13.clone.rows_table) | copy-start | bytes 1572868

commit v2 on v0

v2 whole, which is shorter than its diff:
```python
import functools
import math

import jax
import jax.numpy as jnp
import ml_dtypes
import numpy as np
from jax import lax
from jax.experimental import pallas as pl
from jax.experimental.pallas import tpu as pltpu
from jax.sharding import PartitionSpec as P

TH = 256
TW = 512
OV = 32
BR = 4
BC = 32
PR = 64
PC = 128
FR_G = 4
LEDS = 4
HALF = TH // 2
HR = PR // 2
MARGIN = OV // 2
CORE = TW - OV
LANES = 128
BLOCKS = TW // LANES
MESH = pl.DeviceIdType.MESH
STEP = 0.02
F32 = jnp.float32
BF16 = jnp.bfloat16


def split_np(table):
    hi = table.astype(ml_dtypes.bfloat16)
    lo = (table - hi.astype(np.float64)).astype(ml_dtypes.bfloat16)
    return hi, lo


def wave_np(length, band):
    places = np.arange(length)[:, None]
    freqs = np.arange(band)[None, :] - band // 2
    angle = (places * freqs % length) * (2.0 * np.pi / length)
    return np.cos(angle) / math.sqrt(band), np.sin(angle) / math.sqrt(band)


def object_tables():
    re, im = wave_np(TH, TH)
    rows = []
    for parity in (0, 1):
        a, b = re[:HALF, parity::2], im[:HALF, parity::2]
        rows.append(np.stack(split_np(np.block([[a, -b], [b, a]]))))
    re, im = (np.roll(part.T, -MARGIN, axis=1)[:TH] for part in wave_np(TW, TW))
    cols = np.stack([np.stack(split_np(re)), np.stack(split_np(im))], axis=1)
    return np.stack(rows), cols


def band_tables():
    col_re, col_im = (np.roll(part.T, -MARGIN, axis=1) for part in wave_np(TW, PC))
    cols = np.block([[col_re, col_im], [-col_im, col_re]])
    col_hi, col_lo = split_np(cols)
    row_re, row_im = wave_np(TH, PR)
    spread, gather = [], []
    for parity in (0, 1):
        re = row_re[:HALF, parity::2]
        im = row_im[:HALF, parity::2]
        rows_hi, rows_lo = split_np(np.block([[re, -im], [im, re]]))
        spread.append(np.concatenate([rows_hi, rows_hi, rows_lo, rows_lo], axis=1))
        gather.append(np.concatenate([rows_hi.T, rows_lo.T], axis=0))
    return np.stack([col_hi, col_lo]), np.stack(spread), np.stack(gather)


def split(x):
    hi = x.astype(BF16)
    return hi, (x - hi.astype(F32)).astype(BF16)


def dot(a, b):
    return jnp.dot(a, b, preferred_element_type=F32)


def dot_t(a, b):
    return lax.dot_general(a, b, (((1,), (1,)), ((), ())), preferred_element_type=F32)


def box_corner(pat, lrow, lcol, frame, j):
    led = pat[j, frame]
    return lrow[led], lcol[led]


def row_order(index):
    return jnp.where(index < HR, 2 * index, 2 * index - (PR - 1))


def ones_where(condition):
    return jnp.where(condition, 1.0, 0.0).astype(BF16)


def column_select(col):
    x = lax.broadcasted_iota(jnp.int32, (TW, PC), 0)
    v = lax.broadcasted_iota(jnp.int32, (TW, PC), 1)
    return ones_where(x - v == col)


def load_halves(spec, pup, halves, pd):
    for c in (0, 1):
        hi, lo = split(spec[c])
        halves[0, :, c * TW : (c + 1) * TW] = hi
        halves[1, :, c * TW : (c + 1) * TW] = lo
        for parity in (0, 1):
            pd[c, parity * HR : (parity + 1) * HR] = pup[c, pl.ds(parity, HR, stride=2), :]


def forward_frame(f, frame, pat, lrow, lcol, halves, pd, cols, spread, picked, lit, mid, field):
    y = lax.broadcasted_iota(jnp.int32, (PR, TH), 1)
    order = row_order(lax.broadcasted_iota(jnp.int32, (PR, TH), 0))
    corners = [box_corner(pat, lrow, lcol, frame, j) for j in range(LEDS)]
    choose = jnp.concatenate([ones_where(y - order == row) for row, _ in corners], axis=0)
    for h in (0, 1):
        picked[h] = dot(choose, halves[h]).astype(BF16)
    p_re, p_im = pd[0], pd[1]
    for j in range(LEDS):
        rows = pl.ds(j * PR, PR)
        stack = jnp.concatenate(
            [picked[h, rows, c * TW : (c + 1) * TW] for h in (0, 1) for c in (0, 1)], axis=0
        )
        cut = dot(stack, column_select(corners[j][1]))
        b_re = cut[:PR] + cut[2 * PR : 3 * PR]
        b_im = cut[PR : 2 * PR] + cut[3 * PR :]
        lit[rows, :PC] = p_re * b_re - p_im * b_im
        lit[rows, PC:] = p_re * b_im + p_im * b_re
    hi, lo = split(lit[...])
    mid[...] = dot(hi, cols[0]) + dot(lo, cols[0]) + dot(hi, cols[1])
    estimate = None
    for j in range(LEDS):
        parts = []
        for parity in (0, 1):
            rows = pl.ds(j * PR + parity * HR, HR)
            re_hi, re_lo = split(mid[rows, :TW])
            im_hi, im_lo = split(mid[rows, TW:])
            both = jnp.concatenate([re_hi, im_hi, re_lo, im_lo], axis=0)
            parts.append(dot(spread[parity], jnp.concatenate([both, both], axis=0)))
        upper = parts[0] + parts[1]
        lower = parts[0] - parts[1]
        field[f, j, 0, :HALF] = upper[:HALF]
        field[f, j, 0, HALF:] = lower[:HALF]
        field[f, j, 1, :HALF] = upper[HALF:]
        field[f, j, 1, HALF:] = lower[HALF:]
        power = jnp.concatenate(
            [
                upper[:HALF] * upper[:HALF] + upper[HALF:] * upper[HALF:],
                lower[:HALF] * lower[:HALF] + lower[HALF:] * lower[HALF:],
            ],
            axis=0,
        )
        estimate = power if estimate is None else estimate + power
    return estimate


def backward_frame(
    f, frame, misfit, pat, lrow, lcol, pd, cols, gather, field, low, wide, grad
):
    for j in range(LEDS):
        weighted = [misfit * field[f, j, c] for c in (0, 1)]
        for parity in (0, 1):
            mix = [
                w[:HALF] + w[HALF:] if parity == 0 else w[:HALF] - w[HALF:] for w in weighted
            ]
            hi, lo = split(jnp.concatenate(mix, axis=0))
            table = gather[parity]
            first = dot(table, hi)
            total = first[:PR] + first[PR:] + dot(table[:PR], lo)
            rows = pl.ds(j * PR + parity * HR, HR)
            low[rows, :TW] = total[:HR]
            low[rows, TW:] = total[HR:]
    hi, lo = split(low[...])
    grads = dot_t(hi, cols[0]) + dot_t(lo, cols[0]) + dot_t(hi, cols[1])
    p_re, p_im = pd[0], pd[1]
    lane = lax.broadcasted_iota(jnp.int32, (1, LEDS * PR), 1)
    target = row_order(lane & (PR - 1))
    for j in range(LEDS):
        row, col = box_corner(pat, lrow, lcol, frame, j)
        target = target + jnp.where((lane >= j * PR) & (lane < (j + 1) * PR), row, 0)
        rows = pl.ds(j * PR, PR)
        g_re = grads[j * PR : (j + 1) * PR, :PC]
        g_im = grads[j * PR : (j + 1) * PR, PC:]
        re_hi, re_lo = split(p_re * g_re + p_im * g_im)
        im_hi, im_lo = split(p_re * g_im - p_im * g_re)
        stack = jnp.concatenate([re_hi, im_hi, re_lo, im_lo], axis=0)
        placed = dot_t(stack, column_select(col)).astype(BF16)
        for h in (0, 1):
            for c in (0, 1):
                n = 2 * h + c
                wide[h, rows, c * TW : (c + 1) * TW] = placed[n * PR : (n + 1) * PR]
    y = lax.broadcasted_iota(jnp.int32, (TH, LEDS * PR), 0)
    choose = ones_where(y == target)
    total = dot(choose, wide[0]) + dot(choose, wide[1])
    for c in (0, 1):
        for k in range(BLOCKS):
            first = c * TW + k * LANES
            grad[k, c] += total[:, first : first + LANES]


def pack_edge(value, first):
    lane = lax.broadcasted_iota(jnp.int32, (TH // 8, LANES), 1) // MARGIN
    packed = jnp.zeros((TH // 8, LANES), F32)
    for b in range(8):
        piece = value[b * 32 : (b + 1) * 32]
        piece = pltpu.roll(piece, (MARGIN * b - first) % LANES, 1)
        packed = jnp.where(lane == b, piece, packed)
    return packed


def unpack_edge(packed, first):
    return jnp.concatenate(
        [pltpu.roll(packed, (first - MARGIN * b) % LANES, 1) for b in range(8)], axis=0
    )


def dequantize(raw, scales, dequant):
    frames, rows, width = raw.shape
    dequant[:, :LANES] = jnp.zeros((frames * rows, LANES), F32)
    dequant[:, LANES + width :] = jnp.zeros((frames * rows, LANES), F32)
    lane = lax.broadcasted_iota(jnp.int32, (rows, LANES), 1) // BC
    upper = lax.broadcasted_iota(jnp.int32, (rows, LANES), 0) < BR
    blocks = scales.shape[2]
    per = LANES // BC
    for first in range(0, blocks, LANES):
        count = min(LANES, blocks - first)
        for f in range(frames):
            pair = scales[f, :, first : first + count].astype(F32)
            if count < LANES:
                pair = jnp.concatenate([pair, jnp.zeros((2, LANES - count), F32)], axis=1)
            factors = jnp.where(
                upper,
                jnp.broadcast_to(pair[0:1], (rows, LANES)),
                jnp.broadcast_to(pair[1:2], (rows, LANES)),
            )
            for k in range(count // per):
                column = (first // per + k) * LANES
                spread = jnp.take_along_axis(factors, lane + per * k, axis=1)
                codes = raw[f, :, column : column + LANES].astype(F32)
                dequant[f * rows : (f + 1) * rows, LANES + column : 2 * LANES + column] = (
                    codes * spread
                )


def cut_message(dequant, tile):
    start = CORE * tile - MARGIN + LANES
    aligned = pl.multiple_of(start // LANES * LANES, LANES)
    offset = start - aligned + MARGIN
    wide = dequant[:, pl.ds(aligned, TW + LANES)]
    wide = pltpu.roll(wide, TW + LANES - offset, 1)
    lane = lax.broadcasted_iota(jnp.int32, (1, LANES), 1)
    last = jnp.where(lane < LANES - MARGIN, wide[:, TW - LANES : TW], wide[:, TW:])
    return jnp.concatenate([wide[:, : TW - LANES], last], axis=1).astype(BF16)


def centred():
    y = lax.broadcasted_iota(jnp.int32, (TH, 1), 0).astype(F32) - (TH - 1) / 2.0
    lane = lax.broadcasted_iota(jnp.int32, (1, TW), 1)
    x = lane.astype(F32) - (CORE - 1) / 2.0
    return y, x, lane


Y_NORM = float(np.sum((np.arange(TH) - (TH - 1) / 2.0) ** 2) * CORE)
X_NORM = float(np.sum((np.arange(CORE) - (CORE - 1) / 2.0) ** 2) * TH)


def build_columns(half, table):
    lane = lax.broadcasted_iota(jnp.int32, (1, TW), 1)
    sign = (1 - 2 * (lane & 1)).astype(F32)
    for i in (0, 1):
        rows = pl.ds(i * LANES, LANES)
        for h in (0, 1):
            re = half[h, 0, rows, :].astype(F32)
            im = half[h, 1, rows, :].astype(F32)
            for n, factor in ((0, None), (1, sign)):
                a = re if factor is None else re * factor
                b = im if factor is None else im * factor
                upper = pl.ds(n * LANES, LANES)
                lower = pl.ds((2 + n) * LANES, LANES)
                for k in range(BLOCKS):
                    cut = slice(k * LANES, (k + 1) * LANES)
                    table[i, h, k, upper, :LANES] = a[:, cut].astype(BF16)
                    table[i, h, k, upper, LANES:] = b[:, cut].astype(BF16)
                    table[i, h, k, lower, :LANES] = (-b[:, cut]).astype(BF16)
                    table[i, h, k, lower, LANES:] = a[:, cut].astype(BF16)


def object_rows(i, new, rows_table, lhs):
    parts = []
    for parity in (0, 1):
        data = [
            jnp.concatenate(
                [new[k, c, pl.ds(parity, HALF, stride=2), :] for k in (i, i + 2)], axis=1
            )
            for c in (0, 1)
        ]
        hi, lo = split(jnp.concatenate(data, axis=0))
        t_hi, t_lo = rows_table[parity, 0], rows_table[parity, 1]
        parts.append(dot(t_hi, hi) + dot(t_hi, lo) + dot(t_lo, hi))
    for n, value in enumerate((parts[0] + parts[1], parts[0] - parts[1])):
        hi, lo = split(value)
        rows = pl.ds(n * HALF, HALF)
        for h, part in enumerate((hi, lo)):
            lhs[h, rows, : 2 * LANES] = part[:HALF]
            lhs[h, rows, 2 * LANES :] = part[HALF:]


def object_block(i, k, lhs, table):
    hi, lo = lhs[0], lhs[1]
    return dot(hi, table[i, 0, k]) + dot(lo, table[i, 0, k]) + dot(hi, table[i, 1, k])


def update_kernel(
    tiles,
    pat,
    lrow,
    lcol,
    raw_h,
    scales_h,
    flat_h,
    spec_h,
    pup_h,
    cols_h,
    spread_h,
    gather_h,
    rows_h,
    half_h,
    fresh,
    stitched,
    raw,
    scales,
    flat,
    spec,
    pup,
    cols,
    spread,
    gather,
    rows_table,
    half,
    dequant,
    message,
    arrived,
    window,
    gains,
    flat_out,
    flat_in,
    slope_out,
    slope_in,
    halves,
    pd,
    picked,
    lit,
    mid,
    field,
    estimate,
    grad,
    got,
    pair,
    far,
    new,
    table,
    lhs,
    image,
    strip,
    edge_out,
    edge_in,
    load,
    store,
    send,
    recv,
    side_send,
    side_recv,
):
    frames = raw.shape[0]
    rows = raw.shape[1]
    group = lax.axis_index("grp")
    tile = lax.axis_index("tile")
    core = lax.rem(group, 2)
    mate = {"grp": group + 1 - 2 * core}
    partner = {"grp": group + 2 - 4 * lax.div(group, 2)}
    right = {"tile": lax.rem(tile + 1, tiles)}
    left = {"tile": lax.rem(tile + tiles - 1, tiles)}

    def side(number, src, dst, device):
        return pltpu.make_async_remote_copy(
            src_ref=src,
            dst_ref=dst,
            send_sem=side_send.at[number],
            recv_sem=side_recv.at[number],
            device_id=device,
            device_id_type=MESH,
        )

    def block(source, target):
        return pltpu.make_async_remote_copy(
            src_ref=message.at[target],
            dst_ref=arrived.at[source],
            send_sem=send.at[target],
            recv_sem=recv.at[source],
            device_id={"tile": target},
            device_id_type=MESH,
        )

    loads = [
        pltpu.make_async_copy(src, dst, load.at[n])
        for n, (src, dst) in enumerate(
            (
                (raw_h, raw),
                (scales_h, scales),
                (flat_h, flat),
                (spec_h, spec),
                (pup_h, pup),
                (cols_h, cols),
                (spread_h, spread),
                (gather_h, gather),
                (half_h, half),
                (rows_h, rows_table),
            )
        )
    ]
    for copy in loads:
        copy.start()
    barrier = pltpu.get_barrier_semaphore()

    @pl.loop(1, tiles)
    def _(i):
        pl.semaphore_signal(
            barrier, inc=1, device_id={"tile": lax.rem(tile + i, tiles)}, device_id_type=MESH
        )

    for device in (mate, partner):
        pl.semaphore_signal(barrier, inc=1, device_id=device, device_id_type=MESH)

    loads[0].wait()
    loads[1].wait()
    dequantize(raw, scales, dequant)
    pl.semaphore_wait(barrier, tiles + 1)

    @pl.loop(1, tiles)
    def _(i):
        target = lax.rem(tile + i, tiles)
        message[target] = cut_message(dequant, target)
        block(tile, target).start()

    arrived[tile] = cut_message(dequant, tile)
    loads[2].wait()
    for k in range(BLOCKS - 1):
        gains[:, k * LANES : (k + 1) * LANES] = flat[k * LANES : (k + 1) * LANES, :].T
    tail = jnp.concatenate(
        [flat[3 * LANES :, :], jnp.zeros((TW - CORE, TH), F32)], axis=0
    ).T
    gains[:, 3 * LANES :] = tail
    flat_out[0] = pack_edge(tail, 80)
    flat_out[1] = pack_edge(gains[:, :LANES], 0)
    flats = [
        side(0, flat_out.at[0], flat_in.at[0], right),
        side(1, flat_out.at[1], flat_in.at[1], left),
    ]
    for copy in flats:
        copy.start()

    for copy in loads[3:8]:
        copy.wait()
    load_halves(spec, pup, halves, pd)
    first_frame = group * frames

    def forward(f):
        estimate[f] = forward_frame(
            f, first_frame + f, pat, lrow, lcol, halves, pd, cols, spread, picked, lit, mid, field
        )

    pl.loop(0, frames - 1)(forward)
    grad[...] = jnp.zeros_like(grad)
    for copy in loads[8:]:
        copy.wait()
    build_columns(half, table)

    y, x, lane = centred()
    edge = lane[:, 3 * LANES :]
    for copy in flats:
        copy.wait_recv()
    outer = jnp.where(
        edge < CORE + MARGIN, unpack_edge(flat_in[1], 96), unpack_edge(flat_in[0], 112)
    )
    gains[:, 3 * LANES :] = jnp.where(edge < CORE, gains[:, 3 * LANES :], outer)

    @pl.loop(1, tiles + 1)
    def _(i):
        source = lax.rem(tile + tiles - i, tiles)

        @pl.when(i < tiles)
        def _():
            block(source, tile).wait_recv()

        here = pl.ds(pl.multiple_of(source * rows, rows), rows)
        values = arrived[source].astype(F32)
        for f in range(frames):
            window[f, here, :] = values[f * rows : (f + 1) * rows] * gains[here, :]

    inside = (lane < CORE).astype(F32)
    slopes = []
    for f in range(frames):
        flattened = window[f]
        columns = jnp.sum(flattened, axis=0, keepdims=True)
        tilted = jnp.sum(flattened * y, axis=0, keepdims=True)
        slope_y = jnp.sum(tilted * inside, axis=1, keepdims=True) / Y_NORM
        slope_x = jnp.sum(columns * (x * inside), axis=1, keepdims=True) / X_NORM
        slopes.append((slope_y, slope_x))
        slope_out[f : f + 1] = jnp.broadcast_to(slope_y, (1, LANES))
        slope_out[frames + f : frames + f + 1] = jnp.broadcast_to(slope_x, (1, LANES))
    copies = [side(2, slope_out, slope_in.at[0], right), side(3, slope_out, slope_in.at[1], left)]
    for copy in copies:
        copy.start()
    forward(frames - 1)
    for copy in copies:
        copy.wait_recv()
    x_edge = x[:, 3 * LANES :]
    own = edge < CORE
    after = edge < CORE + MARGIN
    blank = ((~own) & after & (tile == tiles - 1)) | ((~after) & (tile == 0))
    for f in range(frames):
        slope_y, slope_x = slopes[f]
        for k in range(BLOCKS - 1):
            cut = slice(k * LANES, (k + 1) * LANES)
            window[f, :, cut] = window[f, :, cut] - slope_y * y - slope_x * x[:, cut]
        row_y = jnp.where(
            own, slope_y, jnp.where(after, slope_in[1, f : f + 1], slope_in[0, f : f + 1])
        )
        row_x = jnp.where(
            own,
            slope_x * x_edge,
            jnp.where(
                after,
                slope_in[1, frames + f : frames + f + 1] * (x_edge - CORE),
                slope_in[0, frames + f : frames + f + 1] * (x_edge - 32.0),
            ),
        )
        value = window[f, :, 3 * LANES :] - row_y * y - row_x
        window[f, :, 3 * LANES :] = jnp.where(blank, 0.0, value)

    @pl.loop(0, frames)
    def _(f):
        misfit = estimate[f] - window[f]
        backward_frame(
            f, first_frame + f, misfit, pat, lrow, lcol, pd, cols, gather, field, mid, picked, grad
        )

    pieces = [(i, c) for i in (0, 1) for c in (0, 1)]
    first = [
        side(4 + n, grad.at[2 - 2 * core + i, c], got.at[i, c], mate)
        for n, (i, c) in enumerate(pieces)
    ]
    for copy in first:
        copy.start()
    second = []
    for n, (i, c) in enumerate(pieces):
        first[n].wait_recv()
        pair[i, c] = grad[2 * core + i, c] + got[i, c]
        second.append(side(8 + n, pair.at[i, c], far.at[i, c], partner))
        second[n].start()
    third = []
    out = []
    for i in (0, 1):
        mine = 2 * core + i
        lanes = pl.ds(pl.multiple_of(mine * LANES, LANES), LANES)
        for c in (0, 1):
            n = 2 * i + c
            second[n].wait_recv()
            new[mine, c] = spec[c, :, lanes] - STEP * (pair[i, c] + far[i, c])
            third.append(side(12 + n, new.at[mine, c], new.at[mine, c], mate))
            third[n].start()
        for c in (0, 1):
            third[2 * i + c].wait_recv()
        for k in (i, i + 2):
            out.append(
                pltpu.make_async_copy(
                    new.at[k], fresh.at[:, :, k * LANES : (k + 1) * LANES], store.at[k]
                )
            )
            out[-1].start()
        object_rows(i, new, rows_table, lhs)
        if i == 0:
            for k in range(BLOCKS):
                image[k] = object_block(i, k, lhs, table)
    image[3] += object_block(1, 3, lhs, table)
    for c in (0, 1):
        value = image[3, :, c * LANES : (c + 1) * LANES]
        edge_out[0, c] = pack_edge(value, 96)
        edge_out[1, c] = pack_edge(value, 112)
    edges = [
        side(16, edge_out.at[0], edge_in.at[0], right),
        side(17, edge_out.at[1], edge_in.at[1], left),
    ]
    for copy in edges:
        copy.start()
    for k in range(BLOCKS - 1):
        image[k] += object_block(1, k, lhs, table)
    for c in (0, 1):
        for k in (1, 2):
            strip[c, k * LANES : (k + 1) * LANES, :] = image[
                k, :, c * LANES : (c + 1) * LANES
            ].T
    place = edge.astype(F32) - float(3 * LANES)
    at_head = (place < MARGIN) & (tile > 0)
    at_tail = (place >= 80) & (place < 96) & (tile < tiles - 1)
    for copy in edges:
        copy.wait_recv()
    for c in (0, 1):
        mine = image[0, :, c * LANES : (c + 1) * LANES]
        other = unpack_edge(edge_in[0, c], 0)
        blend = mine * ((place + 16.5) / OV) + other * ((15.5 - place) / OV)
        strip[c, :LANES, :] = jnp.where(at_head, blend, mine).T
        mine = image[3, :, c * LANES : (c + 1) * LANES]
        other = unpack_edge(edge_in[1, c], 80)
        blend = mine * ((111.5 - place) / OV) + other * ((place - 79.5) / OV)
        strip[c, 3 * LANES :, :] = jnp.where(at_tail, blend, mine).T[: CORE - 3 * LANES]
        out.append(pltpu.make_async_copy(strip.at[c], stitched.at[c], store.at[4 + c]))
        out[-1].start()
    for copy in flats + copies + first + second + third + edges:
        copy.wait_send()

    @pl.loop(1, tiles)
    def _(i):
        block(tile, lax.rem(tile + i, tiles)).wait_send()

    for copy in out:
        copy.wait()


def update(raw, scales, flat, spectrum, pupil, patterns, led_row, led_col):
    tiles = lax.axis_size("tile")
    frames, rows, width = raw.shape
    deep = frames * rows
    tables = [jnp.asarray(t) for t in band_tables() + object_tables()]
    smem = pl.BlockSpec(memory_space=pltpu.SMEM)
    hbm = pl.BlockSpec(memory_space=pltpu.MemorySpace.HBM)
    arrays = [raw, scales, flat, spectrum, pupil] + tables
    small = (TH // 8, LANES)
    part = (2, TH, LANES)
    scratch = [pltpu.VMEM(a.shape, a.dtype) for a in arrays]
    scratch += [
        pltpu.VMEM((deep, width + 2 * LANES), F32),
        pltpu.VMEM((tiles, deep, TW), BF16),
        pltpu.VMEM((tiles, deep, TW), BF16),
        pltpu.VMEM((frames, TH, TW), F32),
        pltpu.VMEM((TH, TW), F32),
        pltpu.VMEM((2,) + small, F32),
        pltpu.VMEM((2,) + small, F32),
        pltpu.VMEM((2 * frames, LANES), F32),
        pltpu.VMEM((2, 2 * frames, LANES), F32),
        pltpu.VMEM((2, TH, 2 * TW), BF16),
        pltpu.VMEM((2, PR, PC), F32),
        pltpu.VMEM((2, LEDS * PR, 2 * TW), BF16),
        pltpu.VMEM((LEDS * PR, 2 * PC), F32),
        pltpu.VMEM((LEDS * PR, 2 * TW), F32),
        pltpu.VMEM((frames, LEDS, 2, TH, TW), F32),
        pltpu.VMEM((frames, TH, TW), F32),
        pltpu.VMEM((BLOCKS,) + part, F32),
        pltpu.VMEM((2,) + part, F32),
        pltpu.VMEM((2,) + part, F32),
        pltpu.VMEM((2,) + part, F32),
        pltpu.VMEM((BLOCKS,) + part, F32),
        pltpu.VMEM((2, 2, BLOCKS, TW, 2 * LANES), BF16),
        pltpu.VMEM((2, TH, TW), BF16),
        pltpu.VMEM((BLOCKS, TH, 2 * LANES), F32),
        pltpu.VMEM((2, CORE, TH), F32),
        pltpu.VMEM((2, 2) + small, F32),
        pltpu.VMEM((2, 2) + small, F32),
        pltpu.SemaphoreType.DMA((10,)),
        pltpu.SemaphoreType.DMA((6,)),
        pltpu.SemaphoreType.DMA((tiles,)),
        pltpu.SemaphoreType.DMA((tiles,)),
        pltpu.SemaphoreType.DMA((18,)),
        pltpu.SemaphoreType.DMA((18,)),
    ]
    return pl.pallas_call(
        functools.partial(update_kernel, tiles),
        in_specs=[smem] * 3 + [hbm] * len(arrays),
        out_specs=[hbm] * 2,
        out_shape=[
            jax.ShapeDtypeStruct((2, TH, TW), F32),
            jax.ShapeDtypeStruct((2, CORE, TH), F32),
        ],
        scratch_shapes=scratch,
        compiler_params=pltpu.CompilerParams(
            collective_id=1, has_side_effects=True, vmem_limit_bytes=62 * 2**20
        ),
        name="update",
    )(patterns, led_row, led_col, *arrays)


def body(raw, scales, flat, spectrum, pupil, patterns, led_row, led_col):
    fresh, stitched = update(
        raw, scales, flat.T, spectrum[0], pupil, patterns.T, led_row, led_col
    )
    return (fresh[None], jnp.swapaxes(stitched, 1, 2))


def solution(mesh):
    return jax.shard_map(
        body,
        mesh=mesh,
        in_specs=(
            P("grp", "tile", None),
            P("grp", "tile", None),
            P(None, "tile"),
            P("tile", None, None, None),
            P(),
            P(),
            P(),
            P(),
        ),
        out_specs=(P("tile", None, None, None), P(None, None, "tile")),
        check_vma=False,
    )
```

time: 114 us -> 72.9 us (0.64)
  waiting for transfers between devices: 26.9 us -> 0 us
  Pallas kernels: 44.7 us -> 68.8 us
  local copies, waits for them, and re-layouts: 19.5 us -> 3.29 us
  starting transfers between devices: 15.1 us -> 0 us
  other arithmetic: 4.75 us -> 0 us
  between operations: 2.18 us -> 0.65 us
    pallas_call x2 -> x1, Pallas kernels: 44.7 us -> 68.8 us  [update(): pl.pallas_call(functools.partial(update_kernel, tiles), in_specs=[smem] *...]
    all_to_all x1 -> x0, waiting for transfers between devices: 15.4 us -> none  [body(): lax.all_to_all(value_blocks.astype(jnp.bfloat16), 'tile', split_axis=2, c...]
    ppermute x2 -> x0, waiting for transfers between devices: 11.5 us -> none  [the longest x1 9.8 us: padded(): lax.ppermute(lax.slice_in_dim(block, 0, width, axis=dim), axis, backward)]
    all_to_all x1 -> x0, starting transfers between devices: 11.3 us -> none  [body(): lax.all_to_all(value_blocks.astype(jnp.bfloat16), 'tile', split_axis=2, c...]
    reshape x2 -> x0, local copies, waits for them, and re-layouts: 5.95 us -> none  [the longest x1 5.93 us: spread_factors(): jnp.repeat(jnp.repeat(coarse.astype(jnp.float32), BR, axis=1), BC, axis=2)]
    broadcast_in_dim x2 -> x0, local copies, waits for them, and re-layouts: 5.65 us -> none  [the longest x1 4.94 us: spread_factors(): jnp.repeat(jnp.repeat(coarse.astype(jnp.float32), BR, axis=1), BC, axis=2)]
    ppermute x2 -> x0, starting transfers between devices: 3.76 us -> none  [the longest x1 2.29 us: padded(): lax.ppermute(lax.slice_in_dim(block, block.shape[dim] - width, None, axis...]
    convert_element_type x2 -> x0, local copies, waits for them, and re-layouts: 3.31 us -> none  [body(): value_blocks.astype(jnp.bfloat16)]
  transfers between devices with their start and end apart: 3 -> 0, of which waited for: 3 -> 0; matrix products, arithmetic and copies ran while one was open for 1% -> 0% of each run, Pallas kernels for 0% -> 0%
where the time goes in v2:
time: 72.9 us; the launch traced here: 72.7 us
  Pallas kernels  68.8 us (94%)
  local copies, waits for them, and re-layouts  3.29 us (5%)
    pallas_call x1, Pallas kernels, update(): pl.pallas_call(functools.partial(update_kernel, tiles), in_specs=[smem] *...  68.8 us
    unnamed x4, local copies, waits for them, and re-layouts  3.29 us

profile of v2, /device:TPU:1, one launch (start us, length us, event | category | flops | bytes accessed | tf_op | source)
XLA Modules:
  0.0 72.7 jit_solution(15381345731827976684)
XLA Ops:
  0.6 68.8 %update.1 = (f32[2,256,512]{2,1,0:T(8,128)}, f32[2,480,256]{2,1,0:T(8,128)}) custom-call(s32[4,16]{1,0:T(4,128)} %bitcast.9, s32[32]{0:T(128)} %lrow.1, s32[32]{0:T(128)} %lcol.1, bf16[4,8,15360]{2,1,0:T(8,128)(2,1)} %raw_h.1, bf16[4,2,480]{2,1,0:T(2,128)(2,1)} %scales_h.1, f32[480,256]{1,0:T(8,128)} %bitcast.8, f32[2,256,512]{2,1,0:T(8,128)} %bitcast.6, ...), custom_call_target="tpu_custom_call" | custom-call | tf_op jit(solution)/shard_map/update/pallas_call | solution.py:679
  69.4 0.0 copy-start
  69.4 2.3 %copy.17 = f32[1,2,256,512]{3,2,1,0:T(8,128)} copy(f32[1,2,256,512]{3,2,1,0:T(8,128)} %bitcast.5) | data formatting | bytes 2097152
  71.7 0.0 copy-done
  71.8 0.9 %copy.18 = f32[2,256,480]{1,2,0:T(8,128)} copy(f32[2,256,480]{1,2,0:T(8,128)S(1)} %bitcast.7) | data formatting | bytes 1966080
Async XLA Ops:
  69.4 2.4 %copy-start = (f32[2,480,256]{2,1,0:T(8,128)S(1)}, f32[2,480,256]{2,1,0:T(8,128)}, u32[]{:S(2)}) copy-start(f32[2,480,256]{2,1,0:T(8,128)} %get-tuple-element.5) | copy-start | bytes 2949124

commit v3 on v2

--- a/solution.py
+++ b/solution.py
@@ -26,6 +26,8 @@
 LANES = 128
 BLOCKS = TW // LANES
 MESH = pl.DeviceIdType.MESH
+CODE_ROWS = 32
+CODE_TOP = 32767.0
 STEP = 0.02
 F32 = jnp.float32
 BF16 = jnp.bfloat16
@@ -56,9 +58,6 @@
 
 
 def band_tables():
-    col_re, col_im = (np.roll(part.T, -MARGIN, axis=1) for part in wave_np(TW, PC))
-    cols = np.block([[col_re, col_im], [-col_im, col_re]])
-    col_hi, col_lo = split_np(cols)
     row_re, row_im = wave_np(TH, PR)
     spread, gather = [], []
     for parity in (0, 1):
@@ -67,7 +66,7 @@
         rows_hi, rows_lo = split_np(np.block([[re, -im], [im, re]]))
         spread.append(np.concatenate([rows_hi, rows_hi, rows_lo, rows_lo], axis=1))
         gather.append(np.concatenate([rows_hi.T, rows_lo.T], axis=0))
-    return np.stack([col_hi, col_lo]), np.stack(spread), np.stack(gather)
+    return np.stack(spread), np.stack(gather)
 
 
 def split(x):
@@ -79,10 +78,6 @@
     return jnp.dot(a, b, preferred_element_type=F32)
 
 
-def dot_t(a, b):
-    return lax.dot_general(a, b, (((1,), (1,)), ((), ())), preferred_element_type=F32)
-
-
 def box_corner(pat, lrow, lcol, frame, j):
     led = pat[j, frame]
     return lrow[led], lcol[led]
@@ -99,6 +94,12 @@
 def column_select(col):
     x = lax.broadcasted_iota(jnp.int32, (TW, PC), 0)
     v = lax.broadcasted_iota(jnp.int32, (TW, PC), 1)
+    return ones_where(x - v == col)
+
+
+def column_place(col):
+    v = lax.broadcasted_iota(jnp.int32, (PC, TW), 0)
+    x = lax.broadcasted_iota(jnp.int32, (PC, TW), 1)
     return ones_where(x - v == col)
 
 
@@ -174,7 +175,7 @@
             low[rows, :TW] = total[:HR]
             low[rows, TW:] = total[HR:]
     hi, lo = split(low[...])
-    grads = dot_t(hi, cols[0]) + dot_t(lo, cols[0]) + dot_t(hi, cols[1])
+    grads = dot(hi, cols[0]) + dot(lo, cols[0]) + dot(hi, cols[1])
     p_re, p_im = pd[0], pd[1]
     lane = lax.broadcasted_iota(jnp.int32, (1, LEDS * PR), 1)
     target = row_order(lane & (PR - 1))
@@ -187,7 +188,7 @@
         re_hi, re_lo = split(p_re * g_re + p_im * g_im)
         im_hi, im_lo = split(p_re * g_im - p_im * g_re)
         stack = jnp.concatenate([re_hi, im_hi, re_lo, im_lo], axis=0)
-        placed = dot_t(stack, column_select(col)).astype(BF16)
+        placed = dot(stack, column_place(col)).astype(BF16)
         for h in (0, 1):
             for c in (0, 1):
                 n = 2 * h + c
@@ -267,6 +268,31 @@
 X_NORM = float(np.sum((np.arange(CORE) - (CORE - 1) / 2.0) ** 2) * TH)
 
 
+def build_band(half, cols, cols_t):
+    lane = lax.broadcasted_iota(jnp.int32, (1, TW), 1)
+    sign = (2 - 4 * (lane & 1)).astype(F32)
+    for h in (0, 1):
+        re, im = (
+            jnp.concatenate(
+                [
+                    half[h, c, TH - PC // 2 :, :].astype(F32) * 2.0,
+                    half[h, c, : PC // 2, :].astype(F32) * sign,
+                ],
+                axis=0,
+            )
+            for c in (0, 1)
+        )
+        cols[h, :PC, :TW] = re.astype(BF16)
+        cols[h, :PC, TW:] = im.astype(BF16)
+        cols[h, PC:, :TW] = (-im).astype(BF16)
+        cols[h, PC:, TW:] = re.astype(BF16)
+        re, im = re.T, im.T
+        cols_t[h, :TW, :PC] = re.astype(BF16)
+        cols_t[h, :TW, PC:] = (-im).astype(BF16)
+        cols_t[h, TW:, :PC] = im.astype(BF16)
+        cols_t[h, TW:, PC:] = re.astype(BF16)
+
+
 def build_columns(half, table):
     lane = lax.broadcasted_iota(jnp.int32, (1, TW), 1)
     sign = (1 - 2 * (lane & 1)).astype(F32)
@@ -313,6 +339,28 @@
     return dot(hi, table[i, 0, k]) + dot(lo, table[i, 0, k]) + dot(hi, table[i, 1, k])
 
 
+def encode(value, code, unit):
+    for g in range(TH // CODE_ROWS):
+        rows = slice(g * CODE_ROWS, (g + 1) * CODE_ROWS)
+        piece = value[rows]
+        top = jnp.max(jnp.abs(piece), axis=0, keepdims=True)
+        unit[g : g + 1] = top * (1.0 / CODE_TOP)
+        ratio = jnp.where(top > 0.0, CODE_TOP / top, 0.0)
+        whole = jnp.clip(jnp.round(piece * ratio), -CODE_TOP, CODE_TOP)
+        code[rows] = whole.astype(jnp.int32).astype(jnp.int16)
+
+
+def decode(code, unit):
+    return jnp.concatenate(
+        [
+            code[g * CODE_ROWS : (g + 1) * CODE_ROWS].astype(jnp.int32).astype(F32)
+            * unit[g : g + 1]
+            for g in range(TH // CODE_ROWS)
+        ],
+        axis=0,
+    )
+
+
 def update_kernel(
     tiles,
     pat,
@@ -323,7 +371,6 @@
     flat_h,
     spec_h,
     pup_h,
-    cols_h,
     spread_h,
     gather_h,
     rows_h,
@@ -335,11 +382,12 @@
     flat,
     spec,
     pup,
-    cols,
     spread,
     gather,
     rows_table,
     half,
+    cols,
+    cols_t,
     dequant,
     message,
     arrived,
@@ -358,8 +406,10 @@
     estimate,
     grad,
     got,
-    pair,
-    far,
+    code,
+    unit,
+    far_code,
+    far_unit,
     new,
     table,
     lhs,
@@ -413,10 +463,9 @@
                 (flat_h, flat),
                 (spec_h, spec),
                 (pup_h, pup),
-                (cols_h, cols),
+                (half_h, half),
                 (spread_h, spread),
                 (gather_h, gather),
-                (half_h, half),
                 (rows_h, rows_table),
             )
         )
@@ -462,9 +511,10 @@
     for copy in flats:
         copy.start()
 
-    for copy in loads[3:8]:
+    for copy in loads[3:9]:
         copy.wait()
     load_halves(spec, pup, halves, pd)
+    build_band(half, cols, cols_t)
     first_frame = group * frames
 
     def forward(f):
@@ -474,8 +524,6 @@
 
     pl.loop(0, frames - 1)(forward)
     grad[...] = jnp.zeros_like(grad)
-    for copy in loads[8:]:
-        copy.wait()
     build_columns(half, table)
 
     y, x, lane = centred()
@@ -545,7 +593,7 @@
     def _(f):
         misfit = estimate[f] - window[f]
         backward_frame(
-            f, first_frame + f, misfit, pat, lrow, lcol, pd, cols, gather, field, mid, picked, grad
+            f, first_frame + f, misfit, pat, lrow, lcol, pd, cols_t, gather, field, mid, picked, grad
         )
 
     pieces = [(i, c) for i in (0, 1) for c in (0, 1)]
@@ -556,10 +604,13 @@
     for copy in first:
         copy.start()
     second = []
+    units = []
     for n, (i, c) in enumerate(pieces):
         first[n].wait_recv()
-        pair[i, c] = grad[2 * core + i, c] + got[i, c]
-        second.append(side(8 + n, pair.at[i, c], far.at[i, c], partner))
+        encode(grad[2 * core + i, c] + got[i, c], code.at[n], unit.at[n])
+        second.append(side(8 + n, code.at[n], far_code.at[n], partner))
+        units.append(side(18 + n, unit.at[n], far_unit.at[n], partner))
+        units[n].start()
         second[n].start()
     third = []
     out = []
@@ -568,8 +619,10 @@
         lanes = pl.ds(pl.multiple_of(mine * LANES, LANES), LANES)
         for c in (0, 1):
             n = 2 * i + c
+            units[n].wait_recv()
             second[n].wait_recv()
-            new[mine, c] = spec[c, :, lanes] - STEP * (pair[i, c] + far[i, c])
+            total = decode(code.at[n], unit.at[n]) + decode(far_code.at[n], far_unit.at[n])
+            new[mine, c] = spec[c, :, lanes] - STEP * total
             third.append(side(12 + n, new.at[mine, c], new.at[mine, c], mate))
             third[n].start()
         for c in (0, 1):
@@ -619,7 +672,7 @@
         strip[c, 3 * LANES :, :] = jnp.where(at_tail, blend, mine).T[: CORE - 3 * LANES]
         out.append(pltpu.make_async_copy(strip.at[c], stitched.at[c], store.at[4 + c]))
         out[-1].start()
-    for copy in flats + copies + first + second + third + edges:
+    for copy in flats + copies + first + second + units + third + edges:
         copy.wait_send()
 
     @pl.loop(1, tiles)
@@ -642,6 +695,8 @@
     part = (2, TH, LANES)
     scratch = [pltpu.VMEM(a.shape, a.dtype) for a in arrays]
     scratch += [
+        pltpu.VMEM((2, 2 * PC, 2 * TW), BF16),
+        pltpu.VMEM((2, 2 * TW, 2 * PC), BF16),
         pltpu.VMEM((deep, width + 2 * LANES), F32),
         pltpu.VMEM((tiles, deep, TW), BF16),
         pltpu.VMEM((tiles, deep, TW), BF16),
@@ -660,8 +715,10 @@
         pltpu.VMEM((frames, TH, TW), F32),
         pltpu.VMEM((BLOCKS,) + part, F32),
         pltpu.VMEM((2,) + part, F32),
-        pltpu.VMEM((2,) + part, F32),
-        pltpu.VMEM((2,) + part, F32),
+        pltpu.VMEM((4, TH, LANES), jnp.int16),
+        pltpu.VMEM((4, TH // CODE_ROWS, LANES), F32),
+        pltpu.VMEM((4, TH, LANES), jnp.int16),
+        pltpu.VMEM((4, TH // CODE_ROWS, LANES), F32),
         pltpu.VMEM((BLOCKS,) + part, F32),
         pltpu.VMEM((2, 2, BLOCKS, TW, 2 * LANES), BF16),
         pltpu.VMEM((2, TH, TW), BF16),
@@ -669,12 +726,12 @@
         pltpu.VMEM((2, CORE, TH), F32),
         pltpu.VMEM((2, 2) + small, F32),
         pltpu.VMEM((2, 2) + small, F32),
-        pltpu.SemaphoreType.DMA((10,)),
+        pltpu.SemaphoreType.DMA((9,)),
         pltpu.SemaphoreType.DMA((6,)),
         pltpu.SemaphoreType.DMA((tiles,)),
         pltpu.SemaphoreType.DMA((tiles,)),
-        pltpu.SemaphoreType.DMA((18,)),
-        pltpu.SemaphoreType.DMA((18,)),
+        pltpu.SemaphoreType.DMA((22,)),
+        pltpu.SemaphoreType.DMA((22,)),
     ]
     return pl.pallas_call(
         functools.partial(update_kernel, tiles),
@@ -692,10 +749,35 @@
     )(patterns, led_row, led_col, *arrays)
 
 
+def hand_over(first, second, first_out, second_out, sem):
+    copies = [
+        pltpu.make_async_copy(src.at[c], dst.at[c], sem.at[2 * n + c])
+        for n, (src, dst) in enumerate(((first, first_out), (second, second_out)))
+        for c in (0, 1)
+    ]
+    for copy in copies:
+        copy.start()
+    for copy in copies:
+        copy.wait()
+
+
+def deliver(fresh, stitched):
+    hbm = pl.BlockSpec(memory_space=pltpu.MemorySpace.HBM)
+    return pl.pallas_call(
+        hand_over,
+        in_specs=[pl.BlockSpec(memory_space=pl.ANY)] * 2,
+        out_specs=[hbm] * 2,
+        out_shape=[jax.ShapeDtypeStruct(a.shape, a.dtype) for a in (fresh, stitched)],
+        scratch_shapes=[pltpu.SemaphoreType.DMA((4,))],
+        name="deliver",
+    )(fresh, stitched)
+
+
 def body(raw, scales, flat, spectrum, pupil, patterns, led_row, led_col):
     fresh, stitched = update(
         raw, scales, flat.T, spectrum[0], pupil, patterns.T, led_row, led_col
     )
+    fresh, stitched = deliver(fresh, stitched)
     return (fresh[None], jnp.swapaxes(stitched, 1, 2))
 
 

time: 72.9 us -> 129 us (1.77)
  Pallas kernels: 68.8 us -> 128 us
  local copies, waits for them, and re-layouts: 3.29 us -> 0 us
    pallas_call x0 -> x1, Pallas kernels: none -> 62.7 us  [deliver(): pl.pallas_call(hand_over, in_specs=[pl.BlockSpec(memory_space=pl.ANY)] *...]
    pallas_call x1, Pallas kernels: 68.8 us -> 64.9 us  [update(): pl.pallas_call(functools.partial(update_kernel, tiles), in_specs=[smem] *...]
    unnamed x4 -> x0, local copies, waits for them, and re-layouts: 3.29 us -> none
where the time goes in v3:
time: 129 us; the launch traced here: 128 us
  Pallas kernels  128 us (99%)
    pallas_call x1, Pallas kernels, update(): pl.pallas_call(functools.partial(update_kernel, tiles), in_specs=[smem] *...  64.9 us
    pallas_call x1, Pallas kernels, deliver(): pl.pallas_call(hand_over, in_specs=[pl.BlockSpec(memory_space=pl.ANY)] *...  62.7 us

profile of v3, /device:TPU:1, one launch (start us, length us, event | category | flops | bytes accessed | tf_op | source)
XLA Modules:
  0.0 128.4 jit_solution(18126476087714254483)
XLA Ops:
  0.6 64.9 %update.1 = (f32[2,256,512]{2,1,0:T(8,128)}, f32[2,480,256]{2,1,0:T(8,128)}) custom-call(s32[4,16]{1,0:T(4,128)} %bitcast.7, s32[32]{0:T(128)} %lrow.1, s32[32]{0:T(128)} %lcol.1, bf16[4,8,15360]{2,1,0:T(8,128)(2,1)} %raw_h.1, bf16[4,2,480]{2,1,0:T(2,128)(2,1)} %scales_h.1, f32[480,256]{1,0:T(8,128)} %bitcast.6, f32[2,256,512]{2,1,0:T(8,128)} %bitcast.5, ...), custom_call_target="tpu_custom_call" | custom-call | tf_op jit(solution)/shard_map/update/pallas_call | solution.py:736
  65.5 62.7 %deliver.1 = (f32[2,256,512]{2,1,0:T(8,128)}, f32[2,480,256]{2,1,0:T(8,128)}) custom-call(f32[2,256,512]{2,1,0:T(8,128)} %get-tuple-element.6.first, f32[2,480,256]{2,1,0:T(8,128)} %get-tuple-element.7.second), custom_call_target="tpu_custom_call" | custom-call | tf_op jit(solution)/shard_map/deliver/pallas_call | solution.py:766

commit v4 on v3

--- a/solution.py
+++ b/solution.py
@@ -363,9 +363,9 @@
 
 def update_kernel(
     tiles,
-    pat,
-    lrow,
-    lcol,
+    pat_h,
+    lrow_h,
+    lcol_h,
     raw_h,
     scales_h,
     flat_h,
@@ -377,6 +377,9 @@
     half_h,
     fresh,
     stitched,
+    pat,
+    lrow,
+    lcol,
     raw,
     scales,
     flat,
@@ -414,11 +417,9 @@
     table,
     lhs,
     image,
-    strip,
     edge_out,
     edge_in,
     load,
-    store,
     send,
     recv,
     side_send,
@@ -460,6 +461,9 @@
             (
                 (raw_h, raw),
                 (scales_h, scales),
+                (pat_h, pat),
+                (lrow_h, lrow),
+                (lcol_h, lcol),
                 (flat_h, flat),
                 (spec_h, spec),
                 (pup_h, pup),
@@ -495,7 +499,7 @@
         block(tile, target).start()
 
     arrived[tile] = cut_message(dequant, tile)
-    loads[2].wait()
+    loads[5].wait()
     for k in range(BLOCKS - 1):
         gains[:, k * LANES : (k + 1) * LANES] = flat[k * LANES : (k + 1) * LANES, :].T
     tail = jnp.concatenate(
@@ -511,7 +515,7 @@
     for copy in flats:
         copy.start()
 
-    for copy in loads[3:9]:
+    for copy in loads[2:5] + loads[6:]:
         copy.wait()
     load_halves(spec, pup, halves, pd)
     build_band(half, cols, cols_t)
@@ -613,7 +617,6 @@
         units[n].start()
         second[n].start()
     third = []
-    out = []
     for i in (0, 1):
         mine = 2 * core + i
         lanes = pl.ds(pl.multiple_of(mine * LANES, LANES), LANES)
@@ -628,12 +631,7 @@
         for c in (0, 1):
             third[2 * i + c].wait_recv()
         for k in (i, i + 2):
-            out.append(
-                pltpu.make_async_copy(
-                    new.at[k], fresh.at[:, :, k * LANES : (k + 1) * LANES], store.at[k]
-                )
-            )
-            out[-1].start()
+            fresh[:, :, k * LANES : (k + 1) * LANES] = new[k]
         object_rows(i, new, rows_table, lhs)
         if i == 0:
             for k in range(BLOCKS):
@@ -653,7 +651,7 @@
         image[k] += object_block(1, k, lhs, table)
     for c in (0, 1):
         for k in (1, 2):
-            strip[c, k * LANES : (k + 1) * LANES, :] = image[
+            stitched[c, k * LANES : (k + 1) * LANES, :] = image[
                 k, :, c * LANES : (c + 1) * LANES
             ].T
     place = edge.astype(F32) - float(3 * LANES)
@@ -665,22 +663,17 @@
         mine = image[0, :, c * LANES : (c + 1) * LANES]
         other = unpack_edge(edge_in[0, c], 0)
         blend = mine * ((place + 16.5) / OV) + other * ((15.5 - place) / OV)
-        strip[c, :LANES, :] = jnp.where(at_head, blend, mine).T
+        stitched[c, :LANES, :] = jnp.where(at_head, blend, mine).T
         mine = image[3, :, c * LANES : (c + 1) * LANES]
         other = unpack_edge(edge_in[1, c], 80)
         blend = mine * ((111.5 - place) / OV) + other * ((place - 79.5) / OV)
-        strip[c, 3 * LANES :, :] = jnp.where(at_tail, blend, mine).T[: CORE - 3 * LANES]
-        out.append(pltpu.make_async_copy(strip.at[c], stitched.at[c], store.at[4 + c]))
-        out[-1].start()
+        stitched[c, 3 * LANES :, :] = jnp.where(at_tail, blend, mine).T[: CORE - 3 * LANES]
     for copy in flats + copies + first + second + units + third + edges:
         copy.wait_send()
 
     @pl.loop(1, tiles)
     def _(i):
         block(tile, lax.rem(tile + i, tiles)).wait_send()
-
-    for copy in out:
-        copy.wait()
 
 
 def update(raw, scales, flat, spectrum, pupil, patterns, led_row, led_col):
@@ -688,12 +681,16 @@
     frames, rows, width = raw.shape
     deep = frames * rows
     tables = [jnp.asarray(t) for t in band_tables() + object_tables()]
-    smem = pl.BlockSpec(memory_space=pltpu.SMEM)
+    picks = [patterns, led_row, led_col]
     hbm = pl.BlockSpec(memory_space=pltpu.MemorySpace.HBM)
-    arrays = [raw, scales, flat, spectrum, pupil] + tables
+    arrays = [
+        pltpu.with_memory_space_constraint(a, pltpu.MemorySpace.HBM)
+        for a in picks + [raw, scales, flat, spectrum, pupil] + tables
+    ]
     small = (TH // 8, LANES)
     part = (2, TH, LANES)
-    scratch = [pltpu.VMEM(a.shape, a.dtype) for a in arrays]
+    scratch = [pltpu.SMEM(a.shape, a.dtype) for a in picks]
+    scratch += [pltpu.VMEM(a.shape, a.dtype) for a in arrays[3:]]
     scratch += [
         pltpu.VMEM((2, 2 * PC, 2 * TW), BF16),
         pltpu.VMEM((2, 2 * TW, 2 * PC), BF16),
@@ -723,11 +720,9 @@
         pltpu.VMEM((2, 2, BLOCKS, TW, 2 * LANES), BF16),
         pltpu.VMEM((2, TH, TW), BF16),
         pltpu.VMEM((BLOCKS, TH, 2 * LANES), F32),
-        pltpu.VMEM((2, CORE, TH), F32),
         pltpu.VMEM((2, 2) + small, F32),
         pltpu.VMEM((2, 2) + small, F32),
-        pltpu.SemaphoreType.DMA((9,)),
-        pltpu.SemaphoreType.DMA((6,)),
+        pltpu.SemaphoreType.DMA((12,)),
         pltpu.SemaphoreType.DMA((tiles,)),
         pltpu.SemaphoreType.DMA((tiles,)),
         pltpu.SemaphoreType.DMA((22,)),
@@ -735,18 +730,18 @@
     ]
     return pl.pallas_call(
         functools.partial(update_kernel, tiles),
-        in_specs=[smem] * 3 + [hbm] * len(arrays),
-        out_specs=[hbm] * 2,
+        in_specs=[hbm] * len(arrays),
+        out_specs=[pl.BlockSpec(memory_space=pltpu.VMEM)] * 2,
         out_shape=[
             jax.ShapeDtypeStruct((2, TH, TW), F32),
             jax.ShapeDtypeStruct((2, CORE, TH), F32),
         ],
         scratch_shapes=scratch,
         compiler_params=pltpu.CompilerParams(
-            collective_id=1, has_side_effects=True, vmem_limit_bytes=62 * 2**20
+            collective_id=1, has_side_effects=True, vmem_limit_bytes=48 * 2**20
         ),
         name="update",
-    )(patterns, led_row, led_col, *arrays)
+    )(*arrays)
 
 
 def hand_over(first, second, first_out, second_out, sem):
@@ -765,10 +760,11 @@
     hbm = pl.BlockSpec(memory_space=pltpu.MemorySpace.HBM)
     return pl.pallas_call(
         hand_over,
-        in_specs=[pl.BlockSpec(memory_space=pl.ANY)] * 2,
+        in_specs=[pl.BlockSpec(memory_space=pltpu.VMEM)] * 2,
         out_specs=[hbm] * 2,
         out_shape=[jax.ShapeDtypeStruct(a.shape, a.dtype) for a in (fresh, stitched)],
         scratch_shapes=[pltpu.SemaphoreType.DMA((4,))],
+        compiler_params=pltpu.CompilerParams(vmem_limit_bytes=4 * 2**20),
         name="deliver",
     )(fresh, stitched)
 

time: 129 us -> 65.9 us (0.51)
  Pallas kernels: 128 us -> 65 us
    pallas_call x2, Pallas kernels: 128 us -> 65 us  [the longest x1 63.7 us: update(): pl.pallas_call(functools.partial(update_kernel, tiles), in_specs=[hbm] *...]
where the time goes in v4:
time: 65.9 us; the launch traced here: 65.8 us
  Pallas kernels  65 us (99%)
  between operations  0.8 us (1%)
    pallas_call x1, Pallas kernels, update(): pl.pallas_call(functools.partial(update_kernel, tiles), in_specs=[hbm] *...  63.7 us
    pallas_call x1, Pallas kernels, deliver(): pl.pallas_call(hand_over, in_specs=[pl.BlockSpec(memory_space=pltpu.VMEM)...  1.32 us

profile of v4, /device:TPU:1, one launch (start us, length us, event | category | flops | bytes accessed | tf_op | source)
XLA Modules:
  0.0 65.8 jit_solution(10424200096635170200)
XLA Ops:
  0.6 63.7 %update.1 = (f32[2,256,512]{2,1,0:T(8,128)S(1)}, f32[2,480,256]{2,1,0:T(8,128)S(1)}) custom-call(s32[4,16]{1,0:T(4,128)} %bitcast.7, s32[32]{0:T(128)} %lrow_h.1, s32[32]{0:T(128)} %lcol_h.1, bf16[4,8,15360]{2,1,0:T(8,128)(2,1)} %raw_h.1, bf16[4,2,480]{2,1,0:T(2,128)(2,1)} %scales_h.1, f32[480,256]{1,0:T(8,128)} %bitcast.6, f32[2,256,512]{2,1,0:T(8,128)} %bitcast.5, ...), custom_call_target="tpu_custom_call" | custom-call | tf_op jit(solution)/shard_map/update/pallas_call | solution.py:731
  64.3 1.3 %deliver.1 = (f32[2,256,512]{2,1,0:T(8,128)}, f32[2,480,256]{2,1,0:T(8,128)}) custom-call(f32[2,256,512]{2,1,0:T(8,128)S(1)} %get-tuple-element.6.first, f32[2,480,256]{2,1,0:T(8,128)S(1)} %get-tuple-element.7.second), custom_call_target="tpu_custom_call" | custom-call | tf_op jit(solution)/shard_map/deliver/pallas_call | solution.py:761

commit v5 on v4

--- a/solution.py
+++ b/solution.py
@@ -59,14 +59,15 @@
 
 def band_tables():
     row_re, row_im = wave_np(TH, PR)
-    spread, gather = [], []
+    spread = []
     for parity in (0, 1):
         re = row_re[:HALF, parity::2]
         im = row_im[:HALF, parity::2]
         rows_hi, rows_lo = split_np(np.block([[re, -im], [im, re]]))
         spread.append(np.concatenate([rows_hi, rows_hi, rows_lo, rows_lo], axis=1))
-        gather.append(np.concatenate([rows_hi.T, rows_lo.T], axis=0))
-    return np.stack(spread), np.stack(gather)
+    order = np.concatenate([np.arange(0, PR, 2), np.arange(1, PR, 2)])
+    gather = np.concatenate(split_np(np.concatenate([row_re.T[order], row_im.T[order]])))
+    return np.stack(spread), gather
 
 
 def split(x):
@@ -99,6 +100,7 @@
 
 def column_place(col):
     v = lax.broadcasted_iota(jnp.int32, (PC, TW), 0)
+    v = jnp.where(v < PC // 2, 2 * v, 2 * v - (PC - 1))
     x = lax.broadcasted_iota(jnp.int32, (PC, TW), 1)
     return ones_where(x - v == col)
 
@@ -118,7 +120,7 @@
     corners = [box_corner(pat, lrow, lcol, frame, j) for j in range(LEDS)]
     choose = jnp.concatenate([ones_where(y - order == row) for row, _ in corners], axis=0)
     for h in (0, 1):
-        picked[h] = dot(choose, halves[h]).astype(BF16)
+        picked[h, : LEDS * PR] = dot(choose, halves[h]).astype(BF16)
     p_re, p_im = pd[0], pd[1]
     for j in range(LEDS):
         rows = pl.ds(j * PR, PR)
@@ -158,48 +160,67 @@
     return estimate
 
 
-def backward_frame(
-    f, frame, misfit, pat, lrow, lcol, pd, cols, gather, field, low, wide, grad
-):
+def backward_frame(f, frame, misfit, pat, lrow, lcol, pairs, fold, gather, field, bands, wide):
     for j in range(LEDS):
         weighted = [misfit * field[f, j, c] for c in (0, 1)]
         for parity in (0, 1):
             mix = [
-                w[:HALF] + w[HALF:] if parity == 0 else w[:HALF] - w[HALF:] for w in weighted
+                w[:, :TH] + w[:, TH:] if parity == 0 else w[:, :TH] - w[:, TH:]
+                for w in weighted
             ]
-            hi, lo = split(jnp.concatenate(mix, axis=0))
-            table = gather[parity]
-            first = dot(table, hi)
-            total = first[:PR] + first[PR:] + dot(table[:PR], lo)
-            rows = pl.ds(j * PR + parity * HR, HR)
-            low[rows, :TW] = total[:HR]
-            low[rows, TW:] = total[HR:]
-    hi, lo = split(low[...])
-    grads = dot(hi, cols[0]) + dot(lo, cols[0]) + dot(hi, cols[1])
-    p_re, p_im = pd[0], pd[1]
-    lane = lax.broadcasted_iota(jnp.int32, (1, LEDS * PR), 1)
-    target = row_order(lane & (PR - 1))
+            hi, lo = split(jnp.concatenate(mix, axis=1))
+            first = dot(hi, fold[parity])
+            total = first[:, :LANES] + first[:, LANES:] + dot(lo, fold[parity, :, :LANES])
+            hi, lo = split(total)
+            cut = slice((2 * j + parity) * LANES, (2 * j + parity + 1) * LANES)
+            bands[0, :, cut] = hi
+            bands[1, :, cut] = lo
+    first = dot(gather[...], bands[0])
+    second = dot(gather[: 2 * PR], bands[1])
+    by_re = first[:PR] + first[2 * PR : 3 * PR] + second[:PR]
+    by_im = first[PR : 2 * PR] + first[3 * PR :] + second[PR:]
+    left = lax.broadcasted_iota(jnp.int32, (1, LANES), 1) < LANES // 2
+    sign = jnp.where(left, 1.0, -1.0)
+    turn = LANES // 2
     for j in range(LEDS):
-        row, col = box_corner(pat, lrow, lcol, frame, j)
-        target = target + jnp.where((lane >= j * PR) & (lane < (j + 1) * PR), row, 0)
-        rows = pl.ds(j * PR, PR)
-        g_re = grads[j * PR : (j + 1) * PR, :PC]
-        g_im = grads[j * PR : (j + 1) * PR, PC:]
-        re_hi, re_lo = split(p_re * g_re + p_im * g_im)
-        im_hi, im_lo = split(p_re * g_im - p_im * g_re)
+        col = box_corner(pat, lrow, lcol, frame, j)[1]
+        halves = []
+        for parity in (0, 1):
+            cut = slice((2 * j + parity) * LANES, (2 * j + parity + 1) * LANES)
+            band = by_re[:, cut] + sign * pltpu.roll(by_im[:, cut], turn, 1)
+            halves.append(
+                pairs[0, parity] * band + sign * pairs[1, parity] * pltpu.roll(band, turn, 1)
+            )
+        even, odd = halves
+        re_hi, re_lo = split(jnp.where(left, even, pltpu.roll(odd, turn, 1)))
+        im_hi, im_lo = split(jnp.where(left, pltpu.roll(even, turn, 1), odd))
         stack = jnp.concatenate([re_hi, im_hi, re_lo, im_lo], axis=0)
         placed = dot(stack, column_place(col)).astype(BF16)
+        rows = pl.ds(pl.multiple_of((f * LEDS + j) * PR, PR), PR)
         for h in (0, 1):
             for c in (0, 1):
                 n = 2 * h + c
                 wide[h, rows, c * TW : (c + 1) * TW] = placed[n * PR : (n + 1) * PR]
-    y = lax.broadcasted_iota(jnp.int32, (TH, LEDS * PR), 0)
-    choose = ones_where(y == target)
-    total = dot(choose, wide[0]) + dot(choose, wide[1])
-    for c in (0, 1):
-        for k in range(BLOCKS):
-            first = c * TW + k * LANES
-            grad[k, c] += total[:, first : first + LANES]
+
+
+def place_rows(first_frame, frames, pat, lrow, lcol, wide, grad):
+    total_rows = frames * LEDS * PR
+    lane = lax.broadcasted_iota(jnp.int32, (1, total_rows), 1)
+    box = lane // PR
+    target = row_order(lane & (PR - 1))
+    for f in range(frames):
+        for j in range(LEDS):
+            row = box_corner(pat, lrow, lcol, first_frame + f, j)[0]
+            target = target + jnp.where(box == f * LEDS + j, row, 0)
+    choose = ones_where(lax.broadcasted_iota(jnp.int32, (TH, total_rows), 0) == target)
+    for k in range(BLOCKS):
+        for c in (0, 1):
+            cut = slice(c * TW + k * LANES, c * TW + (k + 1) * LANES)
+            if k % 2 == 0:
+                cut = slice(cut.start, cut.stop + LANES)
+                both = dot(choose, wide[0, :, cut]) + dot(choose, wide[1, :, cut])
+                grad[k, c] = both[:, :LANES]
+                grad[k + 1, c] = both[:, LANES:]
 
 
 def pack_edge(value, first):
@@ -268,9 +289,16 @@
 X_NORM = float(np.sum((np.arange(CORE) - (CORE - 1) / 2.0) ** 2) * TH)
 
 
-def build_band(half, cols, cols_t):
+def parity_pick(parity):
+    v = lax.broadcasted_iota(jnp.int32, (PC, LANES), 0)
+    lane = lax.broadcasted_iota(jnp.int32, (PC, LANES), 1)
+    return ones_where(v == 2 * (lane & (PC // 2 - 1)) + parity)
+
+
+def build_band(half, pd, cols, fold, pairs):
     lane = lax.broadcasted_iota(jnp.int32, (1, TW), 1)
     sign = (2 - 4 * (lane & 1)).astype(F32)
+    left = lane[:, :LANES] < LANES // 2
     for h in (0, 1):
         re, im = (
             jnp.concatenate(
@@ -286,11 +314,18 @@
         cols[h, :PC, TW:] = im.astype(BF16)
         cols[h, PC:, :TW] = (-im).astype(BF16)
         cols[h, PC:, TW:] = re.astype(BF16)
-        re, im = re.T, im.T
-        cols_t[h, :TW, :PC] = re.astype(BF16)
-        cols_t[h, :TW, PC:] = (-im).astype(BF16)
-        cols_t[h, TW:, :PC] = im.astype(BF16)
-        cols_t[h, TW:, PC:] = re.astype(BF16)
+        turned = [part[:, :TH].T.astype(BF16) for part in (re, im)]
+        for parity in (0, 1):
+            a, b = (dot(part, parity_pick(parity)) for part in turned)
+            cut = slice(h * LANES, (h + 1) * LANES)
+            fold[parity, :TH, cut] = jnp.where(left, a, -b).astype(BF16)
+            fold[parity, TH:, cut] = jnp.where(left, b, a).astype(BF16)
+    for c in (0, 1):
+        hi = pd[c].astype(BF16)
+        lo, last = split(pd[c] - hi.astype(F32))
+        for parity in (0, 1):
+            pick = parity_pick(parity)
+            pairs[c, parity] = dot(hi, pick) + dot(lo, pick) + dot(last, pick)
 
 
 def build_columns(half, table):
@@ -390,7 +425,9 @@
     rows_table,
     half,
     cols,
-    cols_t,
+    fold,
+    pairs,
+    bands,
     dequant,
     message,
     arrived,
@@ -402,7 +439,7 @@
     slope_in,
     halves,
     pd,
-    picked,
+    wide,
     lit,
     mid,
     field,
@@ -518,16 +555,15 @@
     for copy in loads[2:5] + loads[6:]:
         copy.wait()
     load_halves(spec, pup, halves, pd)
-    build_band(half, cols, cols_t)
+    build_band(half, pd, cols, fold, pairs)
     first_frame = group * frames
 
     def forward(f):
         estimate[f] = forward_frame(
-            f, first_frame + f, pat, lrow, lcol, halves, pd, cols, spread, picked, lit, mid, field
+            f, first_frame + f, pat, lrow, lcol, halves, pd, cols, spread, wide, lit, mid, field
         )
 
     pl.loop(0, frames - 1)(forward)
-    grad[...] = jnp.zeros_like(grad)
     build_columns(half, table)
 
     y, x, lane = centred()
@@ -597,8 +633,10 @@
     def _(f):
         misfit = estimate[f] - window[f]
         backward_frame(
-            f, first_frame + f, misfit, pat, lrow, lcol, pd, cols_t, gather, field, mid, picked, grad
-        )
+            f, first_frame + f, misfit, pat, lrow, lcol, pairs, fold, gather, field, bands, wide
+        )
+
+    place_rows(first_frame, frames, pat, lrow, lcol, wide, grad)
 
     pieces = [(i, c) for i in (0, 1) for c in (0, 1)]
     first = [
@@ -693,7 +731,9 @@
     scratch += [pltpu.VMEM(a.shape, a.dtype) for a in arrays[3:]]
     scratch += [
         pltpu.VMEM((2, 2 * PC, 2 * TW), BF16),
-        pltpu.VMEM((2, 2 * TW, 2 * PC), BF16),
+        pltpu.VMEM((2, 2 * TH, 2 * LANES), BF16),
+        pltpu.VMEM((2, 2, PR, LANES), F32),
+        pltpu.VMEM((2, TH, 2 * LEDS * LANES), BF16),
         pltpu.VMEM((deep, width + 2 * LANES), F32),
         pltpu.VMEM((tiles, deep, TW), BF16),
         pltpu.VMEM((tiles, deep, TW), BF16),
@@ -705,7 +745,7 @@
         pltpu.VMEM((2, 2 * frames, LANES), F32),
         pltpu.VMEM((2, TH, 2 * TW), BF16),
         pltpu.VMEM((2, PR, PC), F32),
-        pltpu.VMEM((2, LEDS * PR, 2 * TW), BF16),
+        pltpu.VMEM((2, frames * LEDS * PR, 2 * TW), BF16),
         pltpu.VMEM((LEDS * PR, 2 * PC), F32),
         pltpu.VMEM((LEDS * PR, 2 * TW), F32),
         pltpu.VMEM((frames, LEDS, 2, TH, TW), F32),
@@ -738,7 +778,7 @@
         ],
         scratch_shapes=scratch,
         compiler_params=pltpu.CompilerParams(
-            collective_id=1, has_side_effects=True, vmem_limit_bytes=48 * 2**20
+            collective_id=1, has_side_effects=True, vmem_limit_bytes=50 * 2**20
         ),
         name="update",
     )(*arrays)

time: 65.9 us -> 64.6 us (0.980)
  Pallas kernels: 65 us -> 63.7 us
    pallas_call x1, Pallas kernels: 63.7 us -> 62.4 us  [update(): pl.pallas_call(functools.partial(update_kernel, tiles), in_specs=[hbm] *...]
where the time goes in v5:
time: 64.6 us; the launch traced here: 64.5 us
  Pallas kernels  63.7 us (99%)
  between operations  0.8 us (1%)
    pallas_call x1, Pallas kernels, update(): pl.pallas_call(functools.partial(update_kernel, tiles), in_specs=[hbm] *...  62.4 us
    pallas_call x1, Pallas kernels, deliver(): pl.pallas_call(hand_over, in_specs=[pl.BlockSpec(memory_space=pltpu.VMEM)...  1.32 us

profile of v5, /device:TPU:1, one launch (start us, length us, event | category | flops | bytes accessed | tf_op | source)
XLA Modules:
  0.0 64.5 jit_solution(15898283464893881753)
XLA Ops:
  0.6 62.4 %update.1 = (f32[2,256,512]{2,1,0:T(8,128)S(1)}, f32[2,480,256]{2,1,0:T(8,128)S(1)}) custom-call(s32[4,16]{1,0:T(4,128)} %bitcast.7, s32[32]{0:T(128)} %lrow_h.1, s32[32]{0:T(128)} %lcol_h.1, bf16[4,8,15360]{2,1,0:T(8,128)(2,1)} %raw_h.1, bf16[4,2,480]{2,1,0:T(2,128)(2,1)} %scales_h.1, f32[480,256]{1,0:T(8,128)} %bitcast.6, f32[2,256,512]{2,1,0:T(8,128)} %bitcast.5, ...), custom_call_target="tpu_custom_call" | custom-call | tf_op jit(solution)/shard_map/update/pallas_call | solution.py:771
  63.0 1.3 %deliver.1 = (f32[2,256,512]{2,1,0:T(8,128)}, f32[2,480,256]{2,1,0:T(8,128)}) custom-call(f32[2,256,512]{2,1,0:T(8,128)S(1)} %get-tuple-element.6.first, f32[2,480,256]{2,1,0:T(8,128)S(1)} %get-tuple-element.7.second), custom_call_target="tpu_custom_call" | custom-call | tf_op jit(solution)/shard_map/deliver/pallas_call | solution.py:801

commit v6 on v5

--- a/solution.py
+++ b/solution.py
@@ -203,7 +203,7 @@
                 wide[h, rows, c * TW : (c + 1) * TW] = placed[n * PR : (n + 1) * PR]
 
 
-def place_rows(first_frame, frames, pat, lrow, lcol, wide, grad):
+def row_places(first_frame, frames, pat, lrow, lcol):
     total_rows = frames * LEDS * PR
     lane = lax.broadcasted_iota(jnp.int32, (1, total_rows), 1)
     box = lane // PR
@@ -212,15 +212,15 @@
         for j in range(LEDS):
             row = box_corner(pat, lrow, lcol, first_frame + f, j)[0]
             target = target + jnp.where(box == f * LEDS + j, row, 0)
-    choose = ones_where(lax.broadcasted_iota(jnp.int32, (TH, total_rows), 0) == target)
-    for k in range(BLOCKS):
-        for c in (0, 1):
-            cut = slice(c * TW + k * LANES, c * TW + (k + 1) * LANES)
-            if k % 2 == 0:
-                cut = slice(cut.start, cut.stop + LANES)
-                both = dot(choose, wide[0, :, cut]) + dot(choose, wide[1, :, cut])
-                grad[k, c] = both[:, :LANES]
-                grad[k + 1, c] = both[:, LANES:]
+    return ones_where(lax.broadcasted_iota(jnp.int32, (TH, total_rows), 0) == target)
+
+
+def place_pair(which, choose, wide, grad):
+    for c in (0, 1):
+        cut = pl.ds(pl.multiple_of(c * TW + which * (2 * LANES), LANES), 2 * LANES)
+        both = dot(choose, wide[0, :, cut]) + dot(choose, wide[1, :, cut])
+        for n in (0, 1):
+            grad[2 * which + n, c] = both[:, n * LANES : (n + 1) * LANES]
 
 
 def pack_edge(value, first):
@@ -437,6 +437,8 @@
     flat_in,
     slope_out,
     slope_in,
+    sums,
+    coef,
     halves,
     pd,
     wide,
@@ -573,7 +575,13 @@
     outer = jnp.where(
         edge < CORE + MARGIN, unpack_edge(flat_in[1], 96), unpack_edge(flat_in[0], 112)
     )
-    gains[:, 3 * LANES :] = jnp.where(edge < CORE, gains[:, 3 * LANES :], outer)
+    own = edge < CORE
+    after = edge < CORE + MARGIN
+    blank = ((~own) & after & (tile == tiles - 1)) | ((~after) & (tile == 0))
+    gains[:, 3 * LANES :] = jnp.where(
+        blank, 0.0, jnp.where(own, gains[:, 3 * LANES :], outer)
+    )
+    sums[...] = jnp.zeros_like(sums)
 
     @pl.loop(1, tiles + 1)
     def _(i):
@@ -586,14 +594,16 @@
         here = pl.ds(pl.multiple_of(source * rows, rows), rows)
         values = arrived[source].astype(F32)
         for f in range(frames):
-            window[f, here, :] = values[f * rows : (f + 1) * rows] * gains[here, :]
+            flattened = values[f * rows : (f + 1) * rows] * gains[here, :]
+            window[f, here, :] = flattened
+            sums[0, f] += flattened
+            sums[1, f] += flattened * (y[:rows] + (source * rows).astype(F32))
 
     inside = (lane < CORE).astype(F32)
     slopes = []
     for f in range(frames):
-        flattened = window[f]
-        columns = jnp.sum(flattened, axis=0, keepdims=True)
-        tilted = jnp.sum(flattened * y, axis=0, keepdims=True)
+        columns = jnp.sum(sums[0, f], axis=0, keepdims=True)
+        tilted = jnp.sum(sums[1, f], axis=0, keepdims=True)
         slope_y = jnp.sum(tilted * inside, axis=1, keepdims=True) / Y_NORM
         slope_x = jnp.sum(columns * (x * inside), axis=1, keepdims=True) / X_NORM
         slopes.append((slope_y, slope_x))
@@ -606,14 +616,10 @@
     for copy in copies:
         copy.wait_recv()
     x_edge = x[:, 3 * LANES :]
-    own = edge < CORE
-    after = edge < CORE + MARGIN
-    blank = ((~own) & after & (tile == tiles - 1)) | ((~after) & (tile == 0))
     for f in range(frames):
         slope_y, slope_x = slopes[f]
-        for k in range(BLOCKS - 1):
-            cut = slice(k * LANES, (k + 1) * LANES)
-            window[f, :, cut] = window[f, :, cut] - slope_y * y - slope_x * x[:, cut]
+        coef[f, 0:1, : 3 * LANES] = jnp.broadcast_to(slope_y, (1, 3 * LANES))
+        coef[f, 1:2, : 3 * LANES] = slope_x * x[:, : 3 * LANES]
         row_y = jnp.where(
             own, slope_y, jnp.where(after, slope_in[1, f : f + 1], slope_in[0, f : f + 1])
         )
@@ -626,17 +632,18 @@
                 slope_in[0, frames + f : frames + f + 1] * (x_edge - 32.0),
             ),
         )
-        value = window[f, :, 3 * LANES :] - row_y * y - row_x
-        window[f, :, 3 * LANES :] = jnp.where(blank, 0.0, value)
+        coef[f, 0:1, 3 * LANES :] = jnp.where(blank, 0.0, row_y)
+        coef[f, 1:2, 3 * LANES :] = jnp.where(blank, 0.0, row_x)
 
     @pl.loop(0, frames)
     def _(f):
-        misfit = estimate[f] - window[f]
+        misfit = estimate[f] - window[f] + coef[f, 0:1] * y + coef[f, 1:2]
         backward_frame(
             f, first_frame + f, misfit, pat, lrow, lcol, pairs, fold, gather, field, bands, wide
         )
 
-    place_rows(first_frame, frames, pat, lrow, lcol, wide, grad)
+    choose = row_places(first_frame, frames, pat, lrow, lcol)
+    place_pair(1 - core, choose, wide, grad)
 
     pieces = [(i, c) for i in (0, 1) for c in (0, 1)]
     first = [
@@ -645,6 +652,7 @@
     ]
     for copy in first:
         copy.start()
+    place_pair(core, choose, wide, grad)
     second = []
     units = []
     for n, (i, c) in enumerate(pieces):
@@ -743,6 +751,8 @@
         pltpu.VMEM((2,) + small, F32),
         pltpu.VMEM((2 * frames, LANES), F32),
         pltpu.VMEM((2, 2 * frames, LANES), F32),
+        pltpu.VMEM((2, frames, rows, TW), F32),
+        pltpu.VMEM((frames, 8, TW), F32),
         pltpu.VMEM((2, TH, 2 * TW), BF16),
         pltpu.VMEM((2, PR, PC), F32),
         pltpu.VMEM((2, frames * LEDS * PR, 2 * TW), BF16),

time: 64.6 us -> 64.3 us (level)
  no operation moved by 1% of the time
where the time goes in v6:
time: 64.3 us; the launch traced here: 64.2 us
  Pallas kernels  63.4 us (99%)
  between operations  0.8 us (1%)
    pallas_call x1, Pallas kernels, update(): pl.pallas_call(functools.partial(update_kernel, tiles), in_specs=[hbm] *...  62.1 us
    pallas_call x1, Pallas kernels, deliver(): pl.pallas_call(hand_over, in_specs=[pl.BlockSpec(memory_space=pltpu.VMEM)...  1.32 us

profile of v6, /device:TPU:1, one launch (start us, length us, event | category | flops | bytes accessed | tf_op | source)
XLA Modules:
  0.0 64.2 jit_solution(5629180394058402542)
XLA Ops:
  0.6 62.1 %update.1 = (f32[2,256,512]{2,1,0:T(8,128)S(1)}, f32[2,480,256]{2,1,0:T(8,128)S(1)}) custom-call(s32[4,16]{1,0:T(4,128)} %bitcast.7, s32[32]{0:T(128)} %lrow_h.1, s32[32]{0:T(128)} %lcol_h.1, bf16[4,8,15360]{2,1,0:T(8,128)(2,1)} %raw_h.1, bf16[4,2,480]{2,1,0:T(2,128)(2,1)} %scales_h.1, f32[480,256]{1,0:T(8,128)} %bitcast.6, f32[2,256,512]{2,1,0:T(8,128)} %bitcast.5, ...), custom_call_target="tpu_custom_call" | custom-call | tf_op jit(solution)/shard_map/update/pallas_call | solution.py:781
  62.7 1.3 %deliver.1 = (f32[2,256,512]{2,1,0:T(8,128)}, f32[2,480,256]{2,1,0:T(8,128)}) custom-call(f32[2,256,512]{2,1,0:T(8,128)S(1)} %get-tuple-element.6.first, f32[2,480,256]{2,1,0:T(8,128)S(1)} %get-tuple-element.7.second), custom_call_target="tpu_custom_call" | custom-call | tf_op jit(solution)/shard_map/deliver/pallas_call | solution.py:811

commit v7 on v6

--- a/solution.py
+++ b/solution.py
@@ -267,11 +267,11 @@
                 )
 
 
-def cut_message(dequant, tile):
+def cut_message(dequant, tile, h, count):
     start = CORE * tile - MARGIN + LANES
     aligned = pl.multiple_of(start // LANES * LANES, LANES)
     offset = start - aligned + MARGIN
-    wide = dequant[:, pl.ds(aligned, TW + LANES)]
+    wide = dequant[h * count : (h + 1) * count, pl.ds(aligned, TW + LANES)]
     wide = pltpu.roll(wide, TW + LANES - offset, 1)
     lane = lax.broadcasted_iota(jnp.int32, (1, LANES), 1)
     last = jnp.where(lane < LANES - MARGIN, wide[:, TW - LANES : TW], wide[:, TW:])
@@ -484,12 +484,12 @@
             device_id_type=MESH,
         )
 
-    def block(source, target):
+    def block(h, source, target):
         return pltpu.make_async_remote_copy(
-            src_ref=message.at[target],
-            dst_ref=arrived.at[source],
-            send_sem=send.at[target],
-            recv_sem=recv.at[source],
+            src_ref=message.at[h, target],
+            dst_ref=arrived.at[h, source],
+            send_sem=send.at[h, target],
+            recv_sem=recv.at[h, source],
             device_id={"tile": target},
             device_id_type=MESH,
         )
@@ -531,13 +531,18 @@
     dequantize(raw, scales, dequant)
     pl.semaphore_wait(barrier, tiles + 1)
 
-    @pl.loop(1, tiles)
-    def _(i):
-        target = lax.rem(tile + i, tiles)
-        message[target] = cut_message(dequant, target)
-        block(tile, target).start()
-
-    arrived[tile] = cut_message(dequant, tile)
+    each = frames // 2
+
+    for h in (0, 1):
+
+        @pl.loop(1, tiles)
+        def _(i):
+            target = lax.rem(tile + i, tiles)
+            message[h, target] = cut_message(dequant, target, h, each * rows)
+            block(h, tile, target).start()
+
+        arrived[h, tile] = cut_message(dequant, tile, h, each * rows)
+
     loads[5].wait()
     for k in range(BLOCKS - 1):
         gains[:, k * LANES : (k + 1) * LANES] = flat[k * LANES : (k + 1) * LANES, :].T
@@ -565,8 +570,7 @@
             f, first_frame + f, pat, lrow, lcol, halves, pd, cols, spread, wide, lit, mid, field
         )
 
-    pl.loop(0, frames - 1)(forward)
-    build_columns(half, table)
+    pl.loop(0, frames)(forward)
 
     y, x, lane = centred()
     edge = lane[:, 3 * LANES :]
@@ -582,65 +586,86 @@
         blank, 0.0, jnp.where(own, gains[:, 3 * LANES :], outer)
     )
     sums[...] = jnp.zeros_like(sums)
-
-    @pl.loop(1, tiles + 1)
-    def _(i):
-        source = lax.rem(tile + tiles - i, tiles)
-
-        @pl.when(i < tiles)
-        def _():
-            block(source, tile).wait_recv()
-
-        here = pl.ds(pl.multiple_of(source * rows, rows), rows)
-        values = arrived[source].astype(F32)
-        for f in range(frames):
-            flattened = values[f * rows : (f + 1) * rows] * gains[here, :]
-            window[f, here, :] = flattened
-            sums[0, f] += flattened
-            sums[1, f] += flattened * (y[:rows] + (source * rows).astype(F32))
+    slope_out[...] = jnp.zeros_like(slope_out)
 
     inside = (lane < CORE).astype(F32)
-    slopes = []
-    for f in range(frames):
-        columns = jnp.sum(sums[0, f], axis=0, keepdims=True)
-        tilted = jnp.sum(sums[1, f], axis=0, keepdims=True)
-        slope_y = jnp.sum(tilted * inside, axis=1, keepdims=True) / Y_NORM
-        slope_x = jnp.sum(columns * (x * inside), axis=1, keepdims=True) / X_NORM
-        slopes.append((slope_y, slope_x))
-        slope_out[f : f + 1] = jnp.broadcast_to(slope_y, (1, LANES))
-        slope_out[frames + f : frames + f + 1] = jnp.broadcast_to(slope_x, (1, LANES))
-    copies = [side(2, slope_out, slope_in.at[0], right), side(3, slope_out, slope_in.at[1], left)]
-    for copy in copies:
-        copy.start()
-    forward(frames - 1)
-    for copy in copies:
-        copy.wait_recv()
     x_edge = x[:, 3 * LANES :]
-    for f in range(frames):
-        slope_y, slope_x = slopes[f]
-        coef[f, 0:1, : 3 * LANES] = jnp.broadcast_to(slope_y, (1, 3 * LANES))
-        coef[f, 1:2, : 3 * LANES] = slope_x * x[:, : 3 * LANES]
-        row_y = jnp.where(
-            own, slope_y, jnp.where(after, slope_in[1, f : f + 1], slope_in[0, f : f + 1])
-        )
-        row_x = jnp.where(
-            own,
-            slope_x * x_edge,
-            jnp.where(
-                after,
-                slope_in[1, frames + f : frames + f + 1] * (x_edge - CORE),
-                slope_in[0, frames + f : frames + f + 1] * (x_edge - 32.0),
-            ),
-        )
-        coef[f, 0:1, 3 * LANES :] = jnp.where(blank, 0.0, row_y)
-        coef[f, 1:2, 3 * LANES :] = jnp.where(blank, 0.0, row_x)
-
-    @pl.loop(0, frames)
-    def _(f):
-        misfit = estimate[f] - window[f] + coef[f, 0:1] * y + coef[f, 1:2]
-        backward_frame(
-            f, first_frame + f, misfit, pat, lrow, lcol, pairs, fold, gather, field, bands, wide
-        )
+
+    def receive(h):
+        @pl.loop(1, tiles + 1)
+        def _(i):
+            source = lax.rem(tile + tiles - i, tiles)
+
+            @pl.when(i < tiles)
+            def _():
+                block(h, source, tile).wait_recv()
+
+            here = pl.ds(pl.multiple_of(source * rows, rows), rows)
+            values = arrived[h, source].astype(F32)
+            place = y[:rows] + (source * rows).astype(F32)
+            for n in range(each):
+                f = h * each + n
+                flattened = values[n * rows : (n + 1) * rows] * gains[here, :]
+                window[f, here, :] = flattened
+                sums[0, f] += flattened
+                sums[1, f] += flattened * place
+
+        slopes = []
+        for n in range(each):
+            f = h * each + n
+            columns = jnp.sum(sums[0, f], axis=0, keepdims=True)
+            tilted = jnp.sum(sums[1, f], axis=0, keepdims=True)
+            slope_y = jnp.sum(tilted * inside, axis=1, keepdims=True) / Y_NORM
+            slope_x = jnp.sum(columns * (x * inside), axis=1, keepdims=True) / X_NORM
+            slopes.append((slope_y, slope_x))
+            slope_out[h, n : n + 1] = jnp.broadcast_to(slope_y, (1, LANES))
+            slope_out[h, each + n : each + n + 1] = jnp.broadcast_to(slope_x, (1, LANES))
+        number = 2 if h == 0 else 22
+        pair = [
+            side(number, slope_out.at[h], slope_in.at[h, 0], right),
+            side(number + 1, slope_out.at[h], slope_in.at[h, 1], left),
+        ]
+        for copy in pair:
+            copy.start()
+        return slopes, pair
+
+    def backward(h, slopes, pair):
+        for copy in pair:
+            copy.wait_recv()
+        for n in range(each):
+            f = h * each + n
+            slope_y, slope_x = slopes[n]
+            coef[f, 0:1, : 3 * LANES] = jnp.broadcast_to(slope_y, (1, 3 * LANES))
+            coef[f, 1:2, : 3 * LANES] = slope_x * x[:, : 3 * LANES]
+            row_y = jnp.where(
+                own,
+                slope_y,
+                jnp.where(after, slope_in[h, 1, n : n + 1], slope_in[h, 0, n : n + 1]),
+            )
+            row_x = jnp.where(
+                own,
+                slope_x * x_edge,
+                jnp.where(
+                    after,
+                    slope_in[h, 1, each + n : each + n + 1] * (x_edge - CORE),
+                    slope_in[h, 0, each + n : each + n + 1] * (x_edge - 32.0),
+                ),
+            )
+            coef[f, 0:1, 3 * LANES :] = jnp.where(blank, 0.0, row_y)
+            coef[f, 1:2, 3 * LANES :] = jnp.where(blank, 0.0, row_x)
+
+        @pl.loop(h * each, (h + 1) * each)
+        def _(f):
+            misfit = estimate[f] - window[f] + coef[f, 0:1] * y + coef[f, 1:2]
+            backward_frame(
+                f, first_frame + f, misfit, pat, lrow, lcol, pairs, fold, gather, field, bands, wide
+            )
+
+    slopes, copies = receive(0)
+    later_slopes, later = receive(1)
+    backward(0, slopes, copies)
+    backward(1, later_slopes, later)
+    copies = copies + later
 
     choose = row_places(first_frame, frames, pat, lrow, lcol)
     place_pair(1 - core, choose, wide, grad)
@@ -662,6 +687,7 @@
         units.append(side(18 + n, unit.at[n], far_unit.at[n], partner))
         units[n].start()
         second[n].start()
+    build_columns(half, table)
     third = []
     for i in (0, 1):
         mine = 2 * core + i
@@ -717,9 +743,11 @@
     for copy in flats + copies + first + second + units + third + edges:
         copy.wait_send()
 
-    @pl.loop(1, tiles)
-    def _(i):
-        block(tile, lax.rem(tile + i, tiles)).wait_send()
+    for h in (0, 1):
+
+        @pl.loop(1, tiles)
+        def _(i):
+            block(h, tile, lax.rem(tile + i, tiles)).wait_send()
 
 
 def update(raw, scales, flat, spectrum, pupil, patterns, led_row, led_col):
@@ -743,14 +771,14 @@
         pltpu.VMEM((2, 2, PR, LANES), F32),
         pltpu.VMEM((2, TH, 2 * LEDS * LANES), BF16),
         pltpu.VMEM((deep, width + 2 * LANES), F32),
-        pltpu.VMEM((tiles, deep, TW), BF16),
-        pltpu.VMEM((tiles, deep, TW), BF16),
+        pltpu.VMEM((2, tiles, deep // 2, TW), BF16),
+        pltpu.VMEM((2, tiles, deep // 2, TW), BF16),
         pltpu.VMEM((frames, TH, TW), F32),
         pltpu.VMEM((TH, TW), F32),
         pltpu.VMEM((2,) + small, F32),
         pltpu.VMEM((2,) + small, F32),
-        pltpu.VMEM((2 * frames, LANES), F32),
-        pltpu.VMEM((2, 2 * frames, LANES), F32),
+        pltpu.VMEM((2, 8, LANES), F32),
+        pltpu.VMEM((2, 2, 8, LANES), F32),
         pltpu.VMEM((2, frames, rows, TW), F32),
         pltpu.VMEM((frames, 8, TW), F32),
         pltpu.VMEM((2, TH, 2 * TW), BF16),
@@ -773,10 +801,10 @@
         pltpu.VMEM((2, 2) + small, F32),
         pltpu.VMEM((2, 2) + small, F32),
         pltpu.SemaphoreType.DMA((12,)),
-        pltpu.SemaphoreType.DMA((tiles,)),
-        pltpu.SemaphoreType.DMA((tiles,)),
-        pltpu.SemaphoreType.DMA((22,)),
-        pltpu.SemaphoreType.DMA((22,)),
+        pltpu.SemaphoreType.DMA((2, tiles)),
+        pltpu.SemaphoreType.DMA((2, tiles)),
+        pltpu.SemaphoreType.DMA((24,)),
+        pltpu.SemaphoreType.DMA((24,)),
     ]
     return pl.pallas_call(
         functools.partial(update_kernel, tiles),

time: 64.3 us -> 65 us (1.011)
  Pallas kernels: 63.4 us -> 64.1 us
    pallas_call x1, Pallas kernels: 62.1 us -> 62.8 us  [update(): pl.pallas_call(functools.partial(update_kernel, tiles), in_specs=[hbm] *...]
where the time goes in v7:
time: 65 us; the launch traced here: 64.9 us
  Pallas kernels  64.1 us (99%)
  between operations  0.8 us (1%)
    pallas_call x1, Pallas kernels, update(): pl.pallas_call(functools.partial(update_kernel, tiles), in_specs=[hbm] *...  62.8 us
    pallas_call x1, Pallas kernels, deliver(): pl.pallas_call(hand_over, in_specs=[pl.BlockSpec(memory_space=pltpu.VMEM)...  1.32 us

profile of v7, /device:TPU:1, one launch (start us, length us, event | category | flops | bytes accessed | tf_op | source)
XLA Modules:
  0.0 64.9 jit_solution(3197650893462868915)
XLA Ops:
  0.6 62.8 %update.1 = (f32[2,256,512]{2,1,0:T(8,128)S(1)}, f32[2,480,256]{2,1,0:T(8,128)S(1)}) custom-call(s32[4,16]{1,0:T(4,128)} %bitcast.7, s32[32]{0:T(128)} %lrow_h.1, s32[32]{0:T(128)} %lcol_h.1, bf16[4,8,15360]{2,1,0:T(8,128)(2,1)} %raw_h.1, bf16[4,2,480]{2,1,0:T(2,128)(2,1)} %scales_h.1, f32[480,256]{1,0:T(8,128)} %bitcast.6, f32[2,256,512]{2,1,0:T(8,128)} %bitcast.5, ...), custom_call_target="tpu_custom_call" | custom-call | tf_op jit(solution)/shard_map/update/pallas_call | solution.py:809
  63.5 1.3 %deliver.1 = (f32[2,256,512]{2,1,0:T(8,128)}, f32[2,480,256]{2,1,0:T(8,128)}) custom-call(f32[2,256,512]{2,1,0:T(8,128)S(1)} %get-tuple-element.6.first, f32[2,480,256]{2,1,0:T(8,128)S(1)} %get-tuple-element.7.second), custom_call_target="tpu_custom_call" | custom-call | tf_op jit(solution)/shard_map/deliver/pallas_call | solution.py:839

commit v8 on v7

--- a/solution.py
+++ b/solution.py
@@ -570,7 +570,7 @@
             f, first_frame + f, pat, lrow, lcol, halves, pd, cols, spread, wide, lit, mid, field
         )
 
-    pl.loop(0, frames)(forward)
+    pl.loop(0, frames - 1)(forward)
 
     y, x, lane = centred()
     edge = lane[:, 3 * LANES :]
@@ -629,7 +629,7 @@
             copy.start()
         return slopes, pair
 
-    def backward(h, slopes, pair):
+    def settle(h, slopes, pair):
         for copy in pair:
             copy.wait_recv()
         for n in range(each):
@@ -654,7 +654,8 @@
             coef[f, 0:1, 3 * LANES :] = jnp.where(blank, 0.0, row_y)
             coef[f, 1:2, 3 * LANES :] = jnp.where(blank, 0.0, row_x)
 
-        @pl.loop(h * each, (h + 1) * each)
+    def backward(start, stop):
+        @pl.loop(start, stop)
         def _(f):
             misfit = estimate[f] - window[f] + coef[f, 0:1] * y + coef[f, 1:2]
             backward_frame(
@@ -662,9 +663,13 @@
             )
 
     slopes, copies = receive(0)
-    later_slopes, later = receive(1)
-    backward(0, slopes, copies)
-    backward(1, later_slopes, later)
+    forward(frames - 1)
+    settle(0, slopes, copies)
+    backward(0, 1)
+    slopes, later = receive(1)
+    backward(1, each)
+    settle(1, slopes, later)
+    backward(each, frames)
     copies = copies + later
 
     choose = row_places(first_frame, frames, pat, lrow, lcol)

time: 65 us -> 69.7 us (1.072)
  Pallas kernels: 64.1 us -> 68.8 us
    pallas_call x1, Pallas kernels: 62.8 us -> 67.5 us  [update(): pl.pallas_call(functools.partial(update_kernel, tiles), in_specs=[hbm] *...]
where the time goes in v8:
time: 69.7 us; the launch traced here: 69.6 us
  Pallas kernels  68.8 us (99%)
  between operations  0.8 us (1%)
    pallas_call x1, Pallas kernels, update(): pl.pallas_call(functools.partial(update_kernel, tiles), in_specs=[hbm] *...  67.5 us

profile of v8, /device:TPU:1, one launch (start us, length us, event | category | flops | bytes accessed | tf_op | source)
XLA Modules:
  0.0 69.6 jit_solution(9359687278242618352)
XLA Ops:
  0.6 67.5 %update.1 = (f32[2,256,512]{2,1,0:T(8,128)S(1)}, f32[2,480,256]{2,1,0:T(8,128)S(1)}) custom-call(s32[4,16]{1,0:T(4,128)} %bitcast.7, s32[32]{0:T(128)} %lrow_h.1, s32[32]{0:T(128)} %lcol_h.1, bf16[4,8,15360]{2,1,0:T(8,128)(2,1)} %raw_h.1, bf16[4,2,480]{2,1,0:T(2,128)(2,1)} %scales_h.1, f32[480,256]{1,0:T(8,128)} %bitcast.6, f32[2,256,512]{2,1,0:T(8,128)} %bitcast.5, ...), custom_call_target="tpu_custom_call" | custom-call | tf_op jit(solution)/shard_map/update/pallas_call | solution.py:814
  68.1 1.3 %deliver.1 = (f32[2,256,512]{2,1,0:T(8,128)}, f32[2,480,256]{2,1,0:T(8,128)}) custom-call(f32[2,256,512]{2,1,0:T(8,128)S(1)} %get-tuple-element.6.first, f32[2,480,256]{2,1,0:T(8,128)S(1)} %get-tuple-element.7.second), custom_call_target="tpu_custom_call" | custom-call | tf_op jit(solution)/shard_map/deliver/pallas_call | solution.py:844

commit v9 on v6

--- a/solution.py
+++ b/solution.py
@@ -533,7 +533,7 @@
 
     @pl.loop(1, tiles)
     def _(i):
-        target = lax.rem(tile + i, tiles)
+        target = lax.rem(tile + 11 * i, tiles)
         message[target] = cut_message(dequant, target)
         block(tile, target).start()
 
@@ -566,7 +566,6 @@
         )
 
     pl.loop(0, frames - 1)(forward)
-    build_columns(half, table)
 
     y, x, lane = centred()
     edge = lane[:, 3 * LANES :]
@@ -585,7 +584,7 @@
 
     @pl.loop(1, tiles + 1)
     def _(i):
-        source = lax.rem(tile + tiles - i, tiles)
+        source = lax.rem(tile + 11 * (tiles - i), tiles)
 
         @pl.when(i < tiles)
         def _():
@@ -662,6 +661,7 @@
         units.append(side(18 + n, unit.at[n], far_unit.at[n], partner))
         units[n].start()
         second[n].start()
+    build_columns(half, table)
     third = []
     for i in (0, 1):
         mine = 2 * core + i

time: 64.3 us -> 64.3 us (level)
  no operation moved by 1% of the time
where the time goes in v9:
time: 64.3 us; the launch traced here: 64.2 us
  Pallas kernels  63.4 us (99%)
  between operations  0.8 us (1%)
    pallas_call x1, Pallas kernels, update(): pl.pallas_call(functools.partial(update_kernel, tiles), in_specs=[hbm] *...  62 us
    pallas_call x1, Pallas kernels, deliver(): pl.pallas_call(hand_over, in_specs=[pl.BlockSpec(memory_space=pltpu.VMEM)...  1.32 us

profile of v9, /device:TPU:1, one launch (start us, length us, event | category | flops | bytes accessed | tf_op | source)
XLA Modules:
  0.0 64.2 jit_solution(5982438376005231025)
XLA Ops:
  0.6 62.0 %update.1 = (f32[2,256,512]{2,1,0:T(8,128)S(1)}, f32[2,480,256]{2,1,0:T(8,128)S(1)}) custom-call(s32[4,16]{1,0:T(4,128)} %bitcast.7, s32[32]{0:T(128)} %lrow_h.1, s32[32]{0:T(128)} %lcol_h.1, bf16[4,8,15360]{2,1,0:T(8,128)(2,1)} %raw_h.1, bf16[4,2,480]{2,1,0:T(2,128)(2,1)} %scales_h.1, f32[480,256]{1,0:T(8,128)} %bitcast.6, f32[2,256,512]{2,1,0:T(8,128)} %bitcast.5, ...), custom_call_target="tpu_custom_call" | custom-call | tf_op jit(solution)/shard_map/update/pallas_call | solution.py:781
  62.7 1.3 %deliver.1 = (f32[2,256,512]{2,1,0:T(8,128)}, f32[2,480,256]{2,1,0:T(8,128)}) custom-call(f32[2,256,512]{2,1,0:T(8,128)S(1)} %get-tuple-element.6.first, f32[2,480,256]{2,1,0:T(8,128)S(1)} %get-tuple-element.7.second), custom_call_target="tpu_custom_call" | custom-call | tf_op jit(solution)/shard_map/deliver/pallas_call | solution.py:811

commit v10 on v6

--- a/solution.py
+++ b/solution.py
@@ -796,9 +796,14 @@
 
 def hand_over(first, second, first_out, second_out, sem):
     copies = [
-        pltpu.make_async_copy(src.at[c], dst.at[c], sem.at[2 * n + c])
+        pltpu.make_async_copy(
+            src.at[c, q * (src.shape[1] // 4) : (q + 1) * (src.shape[1] // 4)],
+            dst.at[c, q * (src.shape[1] // 4) : (q + 1) * (src.shape[1] // 4)],
+            sem.at[8 * n + 4 * c + q],
+        )
         for n, (src, dst) in enumerate(((first, first_out), (second, second_out)))
         for c in (0, 1)
+        for q in range(4)
     ]
     for copy in copies:
         copy.start()
@@ -813,7 +818,7 @@
         in_specs=[pl.BlockSpec(memory_space=pltpu.VMEM)] * 2,
         out_specs=[hbm] * 2,
         out_shape=[jax.ShapeDtypeStruct(a.shape, a.dtype) for a in (fresh, stitched)],
-        scratch_shapes=[pltpu.SemaphoreType.DMA((4,))],
+        scratch_shapes=[pltpu.SemaphoreType.DMA((16,))],
         compiler_params=pltpu.CompilerParams(vmem_limit_bytes=4 * 2**20),
         name="deliver",
     )(fresh, stitched)

time: 64.3 us -> 64.4 us (level)
  no operation moved by 1% of the time
where the time goes in v10:
time: 64.4 us; the launch traced here: 64.3 us
  Pallas kernels  63.5 us (99%)
  between operations  0.8 us (1%)
    pallas_call x1, Pallas kernels, update(): pl.pallas_call(functools.partial(update_kernel, tiles), in_specs=[hbm] *...  62.1 us
    pallas_call x1, Pallas kernels, deliver(): pl.pallas_call(hand_over, in_specs=[pl.BlockSpec(memory_space=pltpu.VMEM)...  1.42 us

profile of v10, /device:TPU:1, one launch (start us, length us, event | category | flops | bytes accessed | tf_op | source)
XLA Modules:
  0.0 64.3 jit_solution(2846130908818067206)
XLA Ops:
  0.6 62.1 %update.1 = (f32[2,256,512]{2,1,0:T(8,128)S(1)}, f32[2,480,256]{2,1,0:T(8,128)S(1)}) custom-call(s32[4,16]{1,0:T(4,128)} %bitcast.7, s32[32]{0:T(128)} %lrow_h.1, s32[32]{0:T(128)} %lcol_h.1, bf16[4,8,15360]{2,1,0:T(8,128)(2,1)} %raw_h.1, bf16[4,2,480]{2,1,0:T(2,128)(2,1)} %scales_h.1, f32[480,256]{1,0:T(8,128)} %bitcast.6, f32[2,256,512]{2,1,0:T(8,128)} %bitcast.5, ...), custom_call_target="tpu_custom_call" | custom-call | tf_op jit(solution)/shard_map/update/pallas_call | solution.py:781
  62.7 1.4 %deliver.1 = (f32[2,256,512]{2,1,0:T(8,128)}, f32[2,480,256]{2,1,0:T(8,128)}) custom-call(f32[2,256,512]{2,1,0:T(8,128)S(1)} %get-tuple-element.6.first, f32[2,480,256]{2,1,0:T(8,128)S(1)} %get-tuple-element.7.second), custom_call_target="tpu_custom_call" | custom-call | tf_op jit(solution)/shard_map/deliver/pallas_call | solution.py:816
